TPU v7x, 256 devices: a whole 4x4x8 slice. The times are simulated.
256 devices in a mesh: seq: 8 (over z), tensor: 32 (over x, y, core).
Axes of the slice: x: 4, y: 4, z: 8, core: 2. Of those that a mesh axis runs over, the one named last changes fastest.
Arguments:
- tokens: bfloat16 [32768, 1536], P(('seq', 'tensor')), may hold values from -6 to 6
- segment_ids: int32 [32768], P(('seq', 'tensor')), may hold values from 0 to 31, never falling along the last dimension, each value on 1 to 4096 neighbouring positions
- page_table: int32 [8, 256], P('seq'), may hold values from 0 to 255, each once within a row
- attn_gain: float32 [1536], replicated, may hold values from 0.6 to 6
- w_qkv: bfloat16 [1536, 2048], P(None, 'tensor'), may hold values from -0.15625 to 0.15625
- w_out: bfloat16 [1536, 1536], P(None, 'tensor'), may hold values from -0.15625 to 0.15625
- moe_gain: float32 [1536], replicated, may hold values from 0.25 to 1.75
- route_ids: int32 [32768, 4], P(('seq', 'tensor')), may hold values from 0 to 31, all different within a row; in each aligned block of 128 rows (0 to 127, 128 to 255, ...) at most 24 rows name the same one
- route_weight: float32 [32768, 4], P(('seq', 'tensor')), may hold values from 0.05 to 1
- w_gate: bfloat16 [32, 1536, 768], P('tensor'), may hold values from -0.15625 to 0.15625
- w_up: bfloat16 [32, 1536, 768], P('tensor'), may hold values from -0.15625 to 0.15625
- w_down: bfloat16 [32, 768, 1536], P('tensor'), may hold values from -0.21875 to 0.21875
Outputs:
- mixed: bfloat16 [32768, 1536], P(('seq', 'tensor'))
- cache: bfloat16 [2048, 16, 512], P(('seq', 'tensor'))
Inputs may be any that keep to these rules, and one draw needn't show every extreme that they name: `segment_ids`: segment numbers never fall along the tokens; every prompt spans 1 to 4096 tokens and one spans exactly 4096. `page_table`: each row is a permutation of the slots of one block. `route_ids`: each token names 4 different experts; among the rows of one device no expert is named more than 24 times, a bound that some block reaches.
All inputs are finite; a program needn't handle non-finite values.
Results may differ from a plain program's by a relative error of at most 0.012.
The roundings to bfloat16 on the way count: a program that leaves them out, or rounds other values in their place, can miss the bound.
Values may be sent and summed in bfloat16 or wider, within the bound.
A program may use at most 128 MiB of HBM per device.

v0:
```python
import math

import jax
import jax.numpy as jnp
from jax import lax
from jax.sharding import PartitionSpec as P

HEADS = 12
KV_HEADS = 2
HEAD = 128
TOP = 4
PAGE = 16


epsilon = 1e-06


def from_behind(value, axis, by):
    length = lax.axis_size(axis)
    pairs = [(i, i + by) for i in range(length) if 0 <= i + by < length]
    return lax.ppermute(value, axis, pairs)


def rms_scaled(values, scales):
    wide = values.astype(jnp.float32)
    mean_sq = jnp.mean(wide * wide, axis=-1, keepdims=True)
    return (wide * lax.rsqrt(mean_sq + epsilon) * scales).astype(jnp.bfloat16)


def attend(queries, keys_window, values_window, allowed):
    scores = jnp.einsum(
        "qhd,kd->hqk", queries, keys_window, preferred_element_type=jnp.float32
    ) / math.sqrt(queries.shape[-1])
    scores = jnp.where(allowed[None], scores, -jnp.inf)
    highest = jnp.max(scores, axis=-1, keepdims=True)
    weights = jnp.exp(scores - highest)
    totals = jnp.sum(weights, axis=-1, keepdims=True)
    shares = (weights / totals).astype(jnp.bfloat16)
    return jnp.einsum("hqk,kd->qhd", shares, values_window, preferred_element_type=jnp.float32)


def body(
    tokens,
    segment_ids,
    page_table,
    attn_gain,
    w_qkv,
    w_out,
    moe_gain,
    route_ids,
    route_weight,
    w_gate,
    w_up,
    w_down,
):
    tok_rows = tokens.shape[0]
    tensor_size = lax.axis_size("tensor")
    tensor_index = lax.axis_index("tensor")
    seq_index = lax.axis_index("seq")
    block_rows = tok_rows * tensor_size
    normed = rms_scaled(tokens, attn_gain)
    block_normed = lax.all_gather(normed, "tensor", axis=0, tiled=True)
    own_columns = jnp.dot(block_normed, w_qkv, preferred_element_type=jnp.float32).astype(
        jnp.bfloat16
    )
    projected = lax.all_to_all(own_columns, "tensor", split_axis=0, concat_axis=1, tiled=True)
    query_width = HEADS * HEAD
    queries = projected[:, :query_width].reshape(tok_rows, HEADS, HEAD)
    own_kv = projected[:, query_width:]
    block_kv, block_segs = (
        lax.all_gather(own_kv, "tensor", axis=0, tiled=True),
        lax.all_gather(segment_ids, "tensor", axis=0, tiled=True),
    )
    earlier_kv, earlier_seg_block = from_behind((block_kv, block_segs), "seq", 1)
    pages_here = tok_rows // PAGE
    pages_block = block_rows // PAGE
    slot_ids = tensor_index * pages_here + jnp.arange(pages_here, dtype=jnp.int32)
    matches = page_table[0][None, :] == slot_ids[:, None]
    logical = jnp.sum(
        jnp.where(matches, jnp.arange(pages_block, dtype=jnp.int32)[None, :], 0), axis=1
    )
    cache_pages = block_kv.reshape(pages_block, PAGE, block_kv.shape[1])[logical]
    all_kv = jnp.concatenate([earlier_kv, block_kv], axis=0)
    all_segs = jnp.concatenate([earlier_seg_block, block_segs], axis=0)
    window = block_rows + tok_rows
    first_key = tensor_index * tok_rows
    keys_window = lax.dynamic_slice_in_dim(all_kv, first_key, window, 0)
    segs_window = lax.dynamic_slice_in_dim(all_segs, first_key, window, 0)
    key_pos = (seq_index - 1) * block_rows + first_key + jnp.arange(window, dtype=jnp.int32)
    query_pos = seq_index * block_rows + first_key + jnp.arange(tok_rows, dtype=jnp.int32)
    allowed = (
        (segs_window[None, :] == segment_ids[:, None])
        & (key_pos[None, :] <= query_pos[:, None])
        & (key_pos[None, :] >= 0)
    )
    per_group = HEADS // KV_HEADS
    contexts = []
    for kv_group in range(KV_HEADS):
        key_cols = keys_window[:, kv_group * HEAD : (kv_group + 1) * HEAD]
        value_cols = keys_window[:, (KV_HEADS + kv_group) * HEAD : (KV_HEADS + kv_group + 1) * HEAD]
        contexts.append(
            attend(
                queries[:, kv_group * per_group : (kv_group + 1) * per_group],
                key_cols,
                value_cols,
                allowed,
            )
        )
    context = jnp.concatenate(contexts, axis=1).reshape(tok_rows, query_width).astype(jnp.bfloat16)
    attn_out = jnp.dot(
        context,
        lax.all_gather(w_out, "tensor", axis=1, tiled=True),
        preferred_element_type=jnp.float32,
    )
    residual = (tokens.astype(jnp.float32) + attn_out).astype(jnp.bfloat16)
    expert_input = rms_scaled(residual, moe_gain)
    experts_all = w_gate.shape[0] * tensor_size
    capacity = max(2, 3 * tok_rows * TOP // (2 * experts_all))
    flat_routes = route_ids.reshape(-1)
    expert_hits = (
        flat_routes[:, None] == jnp.arange(experts_all, dtype=jnp.int32)[None, :]
    ).astype(jnp.int32)
    earlier_hits = jnp.cumsum(expert_hits, axis=0) - expert_hits
    slot_rank = jnp.sum(earlier_hits * expert_hits, axis=1)
    dest_slot = flat_routes * capacity + slot_rank
    slot_table = (
        jnp.arange(experts_all * capacity, dtype=jnp.int32)[:, None, None]
        == dest_slot.reshape(tok_rows, TOP)[None]
    )
    dispatch = jnp.any(slot_table, axis=2).astype(jnp.bfloat16)
    outgoing = jnp.dot(dispatch, expert_input, preferred_element_type=jnp.float32).astype(
        jnp.bfloat16
    )
    outgoing = outgoing.reshape(experts_all, capacity, expert_input.shape[1])
    arrived = lax.all_to_all(outgoing, "tensor", split_axis=0, concat_axis=0, tiled=True)
    rows_flat = arrived.reshape(-1, arrived.shape[-1])
    gate_out = jnp.dot(rows_flat, w_gate[0], preferred_element_type=jnp.float32)
    up_out = jnp.dot(rows_flat, w_up[0], preferred_element_type=jnp.float32)
    hidden = (jnp.maximum(gate_out, 0.0) * up_out).astype(jnp.bfloat16)
    produced = jnp.dot(hidden, w_down[0], preferred_element_type=jnp.float32).astype(jnp.bfloat16)
    returned = lax.all_to_all(
        produced.reshape(arrived.shape), "tensor", split_axis=0, concat_axis=0, tiled=True
    )
    picked = returned.reshape(-1, returned.shape[-1])[dest_slot].reshape(
        tok_rows, TOP, returned.shape[-1]
    )
    routed_sum = jnp.einsum("tk,tkd->td", route_weight, picked.astype(jnp.float32))
    mixed = (residual.astype(jnp.float32) + routed_sum).astype(jnp.bfloat16)
    return (mixed, cache_pages)


def solution(mesh):
    return jax.shard_map(
        body,
        mesh=mesh,
        in_specs=(
            P(("seq", "tensor"), None),
            P(("seq", "tensor")),
            P("seq", None),
            P(),
            P(None, "tensor"),
            P(None, "tensor"),
            P(),
            P(("seq", "tensor"), None),
            P(("seq", "tensor"), None),
            P("tensor", None, None),
            P("tensor", None, None),
            P("tensor", None, None),
        ),
        out_specs=(P(("seq", "tensor"), None), P(("seq", "tensor"), None, None)),
        check_vma=False,
    )
```

profile of v0, /device:TPU:1, one launch (start us, length us, event | category | flops | bytes accessed | tf_op | source)
XLA Modules:
  0.0 425.7 jit_solution(15672935361811713708)
XLA Ops:
  7.2 1.3 fusion.30
  8.5 1.9 fusion.32
  10.5 72.8 %all-gather.5.cloned.1.call-done = bf16[4096,1536]{1,0:T(8,128)(2,1)} async-done(((bf16[128,1536]{1,0:T(8,128)(2,1)}), bf16[4096,1536]{1,0:T(8,128)(2,1)}) %all-gather.5.cloned.1.call-update) | async-done | bytes 12582928 | tf_op jit(solution)/shard_map/all_gather | solution.py:62
  83.3 8.4 %fusion.23 = bf16[8,32,8,128]{3,2,1,0:T(8,128)(2,1)S(1)} fusion(bf16[4096,1536]{1,0:T(8,128)(2,1)} %all-gather.5.cloned.1.call-done, bf16[1536,64]{0,1:T(8,128)(2,1)} %param.16), kind=kOutput, calls=%fused_computation.38 | convolution fusion | flops 805568512 | bytes 13303808 | tf_op jit(solution)/shard_map/dot_general | solution.py:63
  91.8 0.1 copy.73
  91.9 16.9 %all_to_all.29 = bf16[32,128,64]{1,2,0:T(8,128)(2,1)S(1)} all-to-all(bf16[32,128,64]{1,2,0:T(8,128)(2,1)S(1)} %bitcast.107), channel_id=1, replica_groups=mesh['seq'=8,'tensor'=32] {'tensor'}, dimensions={0} | all-to-all | bytes 1048576 | tf_op jit(solution)/shard_map/all_to_all | solution.py:66
  108.8 0.8 copy.65
  109.6 49.0 %all-gather.7.cloned.1.call-done = bf16[4096,512]{1,0:T(8,128)(2,1)} async-done(((bf16[128,512]{1,0:T(8,128)(2,1)}), bf16[4096,512]{1,0:T(8,128)(2,1)}) %all-gather.7.cloned.1.call-update) | async-done | bytes 4194320 | tf_op jit(solution)/shard_map/all_gather | solution.py:71
  158.6 5.1 %collective-permute-start = (bf16[4096,512]{1,0:T(8,128)(2,1)}, bf16[4096,512]{1,0:T(8,128)(2,1)}, u32[]{:S(2)}, u32[]{:S(2)}) collective-permute-start(bf16[4096,512]{1,0:T(8,128)(2,1)} %all-gather.7.cloned.1.call-done), channel_id=1, source_target_pairs={{0,32},{32,64},{64,96},{96,128},{128,160},{160,192},{192,224},{1,3... | collective-permute-start | bytes 12582920 | tf_op jit(solution)/shard_map/ppermute | solution.py:21
  163.7 20.8 %all-gather = s32[32,1,128]{2,1,0:T(1,128)S(1)} all-gather(s32[1,1,128]{2,1,0:T(1,128)S(1)} %bitcast.115), channel_id=1, replica_groups=mesh['seq'=8,'tensor'=32] {'tensor'}, dimensions={0}, use_global_device_ids=true | all-gather | bytes 16896 | tf_op jit(solution)/shard_map/all_gather | solution.py:72
  184.5 1.3 collective-permute-start.1
  185.9 0.1 copy.52
  186.0 0.1 eq.78
  186.1 0.1 eq.74
  186.2 1.2 reduce-window.6
  187.4 0.2 slice_reduce_fusion
  187.6 0.1 fusion.42
  187.8 0.1 reduce_sum.64
  187.9 0.6 broadcast_multiply_fusion
  188.6 0.9 fusion.22
  189.5 62.6 %collective-permute-done.1 = s32[4096]{0:T(1024)S(1)} collective-permute-done((s32[4096]{0:T(1024)S(1)}, s32[4096]{0:T(1024)S(1)}, u32[]{:S(2)}, u32[]{:S(2)}) %collective-permute-start.1) | collective-permute-done | bytes 16416 | tf_op jit(solution)/shard_map/ppermute | solution.py:21
  252.0 0.1 fusion.44
  252.1 3.7 and_and_fusion
  255.9 5.3 %fusion.12 = bf16[4224,512]{1,0:T(8,128)(2,1)S(1)} fusion(s32[]{:T(128)S(6)} %select_n.35, bf16[4096,512]{1,0:T(8,128)(2,1)} %collective-permute-done, bf16[4096,512]{1,0:T(8,128)(2,1)} %all-gather.7.cloned.1.call-done), kind=kLoop, calls=%fused_computation.23 | loop fusion | flops 8650752 | bytes 12713988 | tf_op jit(solution)/shard_map/concatenate | solution.py:83
  261.2 6.6 %fusion.29 = f32[4224,128,6]{1,0,2:T(8,128)} fusion(bf16[4224,512]{1,0:T(8,128)(2,1)S(1)} %fusion.12, bf16[128,12,128]{0,2,1:T(8,128)(2,1)S(1)} %bitcast.108), kind=kOutput, calls=%fused_computation.49 | convolution fusion | flops 830472192 | bytes 14254080 | tf_op jit(solution)/shard_map/qhd,kd->hqk/dot_general | solution.py:31
  267.8 6.5 %fusion.28 = f32[4224,128,6]{1,0,2:T(8,128)} fusion(bf16[4224,512]{1,0:T(8,128)(2,1)S(1)} %fusion.12, bf16[128,12,128]{0,2,1:T(8,128)(2,1)S(1)} %bitcast.109), kind=kOutput, calls=%fused_computation.46 | convolution fusion | flops 830472192 | bytes 14254080 | tf_op jit(solution)/shard_map/qhd,kd->hqk/dot_general | solution.py:31
  274.3 13.8 %fusion.53 = (f32[6,128]{1,0:T(8,128)S(1)}, f32[6,128,4224]{1,2,0:T(8,128)}) fusion(f32[4224,128,6]{1,0,2:T(8,128)} %fusion.29, pred[128,4224]{0,1:T(8,128)(4,1)S(1)} %and_and_fusion), kind=kOutput, calls=%fused_computation.96 | output fusion | flops 12980351 | bytes 26496000 | tf_op jit(solution)/shard_map/sub | solution.py:36
  288.0 14.0 %fusion.52 = (f32[6,128]{1,0:T(8,128)S(1)}, f32[6,128,4224]{1,2,0:T(8,128)}) fusion(f32[4224,128,6]{1,0,2:T(8,128)} %fusion.28, pred[128,4224]{0,1:T(8,128)(4,1)S(1)} %and_and_fusion), kind=kOutput, calls=%fused_computation.95 | output fusion | flops 12980351 | bytes 26496000 | tf_op jit(solution)/shard_map/sub | solution.py:36
  302.0 5.9 %fusion.26 = bf16[128,6,128]{0,2,1:T(8,128)(2,1)S(1)} fusion(f32[6,128,4224]{1,2,0:T(8,128)} %get-tuple-element.7, f32[6,128]{1,0:T(8,128)S(1)} %get-tuple-element.6, bf16[4224,512]{1,0:T(8,128)(2,1)S(1)} %fusion.12), kind=kOutput, calls=%fused_computation.43 | convolution fusion | flops 837058560 | bytes 14258176 | tf_op jit(solution)/shard_map/hqk,kd->qhd/dot_general | solution.py:39
  308.0 2.4 copy-done.1
  310.4 1.1 fusion.27
  311.5 0.8 pad_maximum_fusion
  312.3 4.2 multiply_reduce_fusion
  316.6 1.9 convolution_convert_fusion.2
  318.5 37.4 %all_to_all.30 = bf16[32,24,1536]{2,1,0:T(8,128)(2,1)S(1)} all-to-all(bf16[32,24,1536]{2,1,0:T(8,128)(2,1)S(1)} %bitcast.100), channel_id=1, replica_groups=mesh['seq'=8,'tensor'=32] {'tensor'}, dimensions={0} | all-to-all | bytes 4718592 | tf_op jit(solution)/shard_map/all_to_all | solution.py:135
  355.9 1.4 copy-done.3
  357.3 3.4 fusion.16
  360.7 9.1 %convolution_convert_fusion.1 = bf16[768,1536]{1,0:T(8,128)(2,1)} fusion(bf16[1,768,1536]{2,1,0:T(8,128)(2,1)S(1)} %copy-done, f32[768,768]{1,0:T(8,128)} %fusion.16, bf16[768,1536]{1,0:T(8,128)(2,1)} %bitcast.104, bf16[1,1536,768]{2,1,0:T(8,128)(2,1)} %param.21), kind=kOutput, calls=%fused_computation.24 | convolution fusion | flops 3626827776 | bytes 11796480 | tf_op jit(solution)/shard_map/dot_general | solution.py:140
  369.8 4.7 %all-to-all-start.2 = ((bf16[32,24,1536]{2,1,0:T(8,128)(2,1)}), bf16[32,24,1536]{2,1,0:T(8,128)(2,1)}, u32[]{:S(2)}, u32[]{:S(2)}) async-start(bf16[32,24,1536]{2,1,0:T(8,128)(2,1)} %bitcast.102), calls=%async_computation.2 | async-start | bytes 4718592 | tf_op jit(solution)/shard_map/all_to_all | solution.py:141
  374.5 0.1 mul.91
  374.7 0.2 copy.61
  374.9 0.2 select_reduce_fusion
  375.1 3.4 gather_fusion.1
  378.5 27.3 %all-to-all-done.2 = bf16[32,24,1536]{2,1,0:T(8,128)(2,1)} async-done(((bf16[32,24,1536]{2,1,0:T(8,128)(2,1)}), bf16[32,24,1536]{2,1,0:T(8,128)(2,1)}, u32[]{:S(2)}, u32[]{:S(2)}) %all-to-all-start.2) | async-done | bytes 2359328 | tf_op jit(solution)/shard_map/all_to_all | solution.py:141
  405.8 6.4 %gather_fusion = bf16[512,1536]{1,0:T(8,128)(2,1)} fusion(bf16[768,1536]{1,0:T(8,128)(2,1)} %bitcast.22, s32[1024]{0:T(1024)S(1)} %pad_clamp_fusion.1), kind=kCustom, calls=%fused_computation | custom fusion | bytes 3147776 | tf_op jit(solution)/shard_map/gather | solution.py:144
  412.1 3.9 reshape.209
  416.0 2.4 fusion.54
  418.4 0.8 fusion.33
  (44 shorter events, 0.4 us)
Async XLA Ops:
  7.2 353.6 %copy-start = (bf16[1,768,1536]{2,1,0:T(8,128)(2,1)S(1)}, bf16[1,768,1536]{2,1,0:T(8,128)(2,1)}, u32[]{:S(2)}) copy-start(bf16[1,768,1536]{2,1,0:T(8,128)(2,1)} %param.23) | copy-start | bytes 7077892
  7.2 76.1 %all-gather.5.cloned.1.call-start = ((), (), s32[]{:S(2)}) async-start(), calls=%async_computation.3 | async-start | bytes 12976128 | tf_op jit(solution)/shard_map/all_gather | solution.py:62
  10.5 153.2 %copy-start.6 = (s32[128]{0:T(128)S(1)}, s32[128]{0:T(128)}, u32[]{:S(2)}) copy-start(s32[128]{0:T(128)} %param.13) | copy-start | bytes 1540
  10.5 175.4 %copy-start.7 = (s32[128,4]{0,1:T(4,128)S(1)}, s32[128,4]{0,1:T(4,128)}, u32[]{:S(2)}) copy-start(s32[128,4]{0,1:T(4,128)} %param.19) | copy-start | bytes 6148
  10.5 148.1 %all-gather.7.cloned.1.call-start = ((), (), s32[]{:S(2)}) async-start(), calls=%async_computation.4 | async-start | bytes 4325376 | tf_op jit(solution)/shard_map/all_gather | solution.py:71
  109.6 202.8 %all-gather.9.cloned.1.call-start = ((), (), s32[]{:S(2)}) async-start(), calls=%async_computation.5 | async-start | bytes 4866048 | tf_op jit(solution)/shard_map/all_gather | solution.py:112
  158.6 97.3 %collective-permute-start = (bf16[4096,512]{1,0:T(8,128)(2,1)}, bf16[4096,512]{1,0:T(8,128)(2,1)}, u32[]{:S(2)}, u32[]{:S(2)}) collective-permute-start(bf16[4096,512]{1,0:T(8,128)(2,1)} %all-gather.7.cloned.1.call-done), channel_id=1, source_target_pairs={{0,32},{32,64},{64,96},{96,128},{128,160},{160,192},{192,224},{1,3... | collective-permute-start | bytes 12582920 | tf_op jit(solution)/shard_map/ppermute | solution.py:21
  184.5 67.5 %collective-permute-start.1 = (s32[4096]{0:T(1024)S(1)}, s32[4096]{0:T(1024)S(1)}, u32[]{:S(2)}, u32[]{:S(2)}) collective-permute-start(s32[4096]{0:T(1024)S(1)} %bitcast.111), channel_id=1, source_target_pairs={{0,32},{32,64},{64,96},{96,128},{128,160},{160,192},{192,224},{1,3... | collective-permute-start | bytes 49160 | tf_op jit(solution)/shard_map/ppermute | solution.py:21
  302.0 8.4 %copy-start.1 = (f32[6,128,4224]{1,2,0:T(8,128)S(1)}, f32[6,128,4224]{1,2,0:T(8,128)}, u32[]{:S(2)}) copy-start(f32[6,128,4224]{1,2,0:T(8,128)} %get-tuple-element.5) | copy-start | bytes 38928388
  310.4 1.9 copy-start.2
  311.5 5.0 %copy-start.5 = (f32[1536]{0:T(1024)S(1)}, f32[1536]{0:T(1024)}, u32[]{:S(2)}) copy-start(f32[1536]{0:T(1024)} %param.18) | copy-start | bytes 18436
  316.5 40.8 %copy-start.10 = (bf16[1,1536,768]{2,1,0:T(8,128)(2,1)S(1)}, bf16[1,1536,768]{2,1,0:T(8,128)(2,1)}, u32[]{:S(2)}) copy-start(bf16[1,1536,768]{2,1,0:T(8,128)(2,1)} %param.22) | copy-start | bytes 7077892
  355.9 1.4 copy-start.3
  369.8 4.7 %copy-start.4 = (s32[128,4]{1,0:T(8,128)S(1)}, s32[128,4]{1,0:T(8,128)}, u32[]{:S(2)}) copy-start(s32[128,4]{1,0:T(8,128)} %get-tuple-element.2) | copy-start | bytes 6148
  369.8 4.9 %copy-start.8 = (f32[128,4]{0,1:T(4,128)S(1)}, f32[128,4]{0,1:T(4,128)}, u32[]{:S(2)}) copy-start(f32[128,4]{0,1:T(4,128)} %param.20) | copy-start | bytes 6148
  369.8 5.1 %copy-start.9 = (s32[1,256]{1,0:T(1,128)S(1)}, s32[1,256]{1,0:T(1,128)}, u32[]{:S(2)}) copy-start(s32[1,256]{1,0:T(1,128)} %param.14) | copy-start | bytes 3076
  369.8 36.0 %all-to-all-start.2 = ((bf16[32,24,1536]{2,1,0:T(8,128)(2,1)}), bf16[32,24,1536]{2,1,0:T(8,128)(2,1)}, u32[]{:S(2)}, u32[]{:S(2)}) async-start(bf16[32,24,1536]{2,1,0:T(8,128)(2,1)} %bitcast.102), calls=%async_computation.2 | async-start | bytes 4718592 | tf_op jit(solution)/shard_map/all_to_all | solution.py:141
Sparse Core Ops, SparseCore 0:
  11.1 72.1 all-gather.4
  109.7 48.8 all-gather.6
  186.0 50.2 all-gather.8
where the time goes:
time: 426 us
  waiting for transfers between devices  212 us (50%)
  blocking collectives  75.1 us (18%)
  matrix products  49.4 us (12%)
  other arithmetic  44.8 us (11%)
  local copies, waits for them, and re-layouts  19.5 us (5%)
  between operations  14 us (3%)
  starting transfers between devices  11.2 us (3%)
    all_gather x1, waiting for transfers between devices, body(): block_normed = lax.all_gather(normed, 'tensor', axis=0, tiled=True)  72.8 us
    ppermute x2, waiting for transfers between devices, from_behind(): return lax.ppermute(value, axis, pairs)  62.6 us
    all_gather x1, waiting for transfers between devices, body(): lax.all_gather(own_kv, 'tensor', axis=0, tiled=True)  49 us
    all_to_all x1, blocking collectives, body(): lax.all_to_all(outgoing, 'tensor', split_axis=0, concat_axis=0, tiled=True)  37.4 us
    sub x2, other arithmetic, attend(): weights = jnp.exp(scores - highest)  27.8 us
    all_to_all x1, waiting for transfers between devices, body(): lax.all_to_all(produced.reshape(arrived.shape), 'tensor', split_axis=0, c...  27.3 us
    all_gather x1, blocking collectives, body(): lax.all_gather(segment_ids, 'tensor', axis=0, tiled=True)  20.8 us
    all_to_all x1, blocking collectives, body(): lax.all_to_all(own_columns, 'tensor', split_axis=0, concat_axis=1, tiled=...  16.9 us
  transfers between devices with their start and end apart: 6, of which 4 were waited for; matrix products, arithmetic and copies ran while one was open for 15% of the time, Pallas kernels for 0%

commit v1 on v0

v1 whole, which is shorter than its diff:
```python
import functools
import math

import jax
import jax.numpy as jnp
from jax import lax
from jax.experimental import pallas as pl
from jax.experimental.pallas import tpu as pltpu
from jax.sharding import PartitionSpec as P

HEADS = 12
KV_HEADS = 2
HEAD = 128
TOP = 4
PAGE = 16
SEGS = 32
CHUNKS = 32
TOK = 128
STEP = 3
NEG = -1e30

epsilon = 1e-06
F32 = jnp.float32
BF16 = jnp.bfloat16


def rms_scaled(values, scales):
    wide = values.astype(F32)
    mean_sq = jnp.mean(wide * wide, axis=-1, keepdims=True)
    return (wide * lax.rsqrt(mean_sq + epsilon) * scales).astype(BF16)


def attention_kernel(starts_ref, q_ref, kv_ref, out_ref, top, total, acc):
    place = lax.axis_index("tensor")
    scale = math.log2(math.e) / math.sqrt(HEAD)
    group_heads = HEADS // KV_HEADS
    top[...] = jnp.full_like(top, NEG)
    total[...] = jnp.zeros_like(total)
    acc[...] = jnp.zeros_like(acc)
    starts = starts_ref[...]
    query = lax.broadcasted_iota(jnp.int32, (STEP * TOK, TOK), 1) + CHUNKS * TOK
    local = lax.broadcasted_iota(jnp.int32, (STEP * TOK, TOK), 0)

    def step(number, _):
        first = number * STEP
        pieces = []
        for i in range(STEP):
            w = place + first + i
            own = w >= CHUNKS
            chunk = jnp.where(own, w - CHUNKS, w)
            row = pl.multiple_of(jnp.where(own, 0, TOK), TOK)
            pieces.append(kv_ref.at[chunk, pl.ds(row, TOK), :])
        pos = local + first * TOK
        allowed = (pos >= starts) & (pos <= query)
        for g in range(KV_HEADS):
            keys = jnp.concatenate([p[:, g * HEAD : (g + 1) * HEAD] for p in pieces], axis=0)
            vals = jnp.concatenate(
                [p[:, (KV_HEADS + g) * HEAD : (KV_HEADS + g + 1) * HEAD] for p in pieces], axis=0
            )
            for h in range(group_heads):
                head = g * group_heads + h
                s = jnp.dot(keys, q_ref[head], preferred_element_type=F32) * scale
                s = jnp.where(allowed, s, NEG)
                old = top[head : head + 1, :]
                new = jnp.maximum(old, jnp.max(s, axis=0, keepdims=True))
                alpha = jnp.exp2(old - new)
                w = jnp.exp2(s - new)
                top[head : head + 1, :] = new
                total[head : head + 1, :] = total[head : head + 1, :] * alpha + jnp.sum(
                    w, axis=0, keepdims=True
                )
                got = lax.dot_general(
                    vals, w.astype(BF16), (((0,), (0,)), ((), ())), preferred_element_type=F32
                )
                acc[head] = acc[head] * alpha + got
        return 0

    lax.fori_loop(0, (CHUNKS + 1) // STEP, step, 0)
    for head in range(HEADS):
        out_ref[head] = (acc[head] / total[head : head + 1, :]).astype(BF16)


def attention(starts, q_t, kv_all):
    vm = pl.BlockSpec(memory_space=pltpu.VMEM)
    return pl.pallas_call(
        attention_kernel,
        out_shape=jax.ShapeDtypeStruct((HEADS, HEAD, TOK), BF16),
        in_specs=[vm, vm, vm],
        out_specs=vm,
        scratch_shapes=[
            pltpu.VMEM((16, TOK), F32),
            pltpu.VMEM((16, TOK), F32),
            pltpu.VMEM((HEADS, HEAD, TOK), F32),
        ],
        cost_estimate=pl.CostEstimate(
            flops=4 * HEADS * TOK * HEAD * (CHUNKS + 1) * TOK,
            bytes_accessed=kv_all.size * 2,
            transcendentals=HEADS * TOK * (CHUNKS + 1) * TOK,
        ),
        name="window_attention",
    )(starts, q_t, kv_all)


def body(
    tokens,
    segment_ids,
    page_table,
    attn_gain,
    w_qkv,
    w_out,
    moe_gain,
    route_ids,
    route_weight,
    w_gate,
    w_up,
    w_down,
):
    tok_rows = tokens.shape[0]
    tensor_size = lax.axis_size("tensor")
    tensor_index = lax.axis_index("tensor")
    seq_index = lax.axis_index("seq")
    seq_size = lax.axis_size("seq")
    query_width = HEADS * HEAD

    counts = jnp.sum(
        (segment_ids[:, None] < jnp.arange(TOK, dtype=jnp.int32)[None, :]).astype(F32), axis=0
    ).astype(BF16)
    counts_rows = jnp.pad(counts[None, :], ((0, PAGE - 1), (0, tokens.shape[1] - TOK)))
    sent = jnp.concatenate([tokens, counts_rows], axis=0)
    earlier = lax.ppermute(sent, "seq", [(i, i + 1) for i in range(seq_size - 1)])
    both = jnp.concatenate([tokens, earlier[:tok_rows]], axis=0)
    normed = rms_scaled(both, attn_gain)
    qkv_t = lax.all_gather(w_qkv.T, "tensor", axis=0, tiled=True)
    nt = (((1,), (1,)), ((), ()))
    q_t = lax.dot_general(
        qkv_t[:query_width], normed[:tok_rows], nt, preferred_element_type=F32
    ).astype(BF16)
    kv = lax.dot_general(normed, qkv_t[query_width:], nt, preferred_element_type=F32).astype(BF16)
    kvw = kv.shape[1]
    seg_rows = jnp.concatenate(
        [jnp.pad(counts[None, :], ((0, 0), (0, kvw - TOK))),
         jnp.pad(earlier[tok_rows:, :kvw], ((0, 0), (0, 0)))[: PAGE - 1]], axis=0
    )
    chunk = jnp.concatenate([kv, seg_rows], axis=0)
    kv_all = lax.all_gather(chunk, "tensor", axis=0, tiled=False)

    own_counts = kv_all[:, 2 * tok_rows, :TOK].astype(F32)
    prev_counts = kv_all[:, 2 * tok_rows + 1, :TOK].astype(F32)
    order = jnp.arange(tensor_size)[:, None]
    before = jnp.where(seq_index == 0, jnp.full_like(prev_counts, TOK), prev_counts)
    starts_of = jnp.sum(
        jnp.where(order <= tensor_index, own_counts, 0.0)
        + jnp.where(order >= tensor_index, before, 0.0),
        axis=0,
    ).astype(jnp.int32)
    starts = jnp.sum(
        jnp.where(
            segment_ids[None, :] == jnp.arange(TOK, dtype=jnp.int32)[:, None], starts_of[:, None], 0
        ),
        axis=0,
    )
    ctx = attention(starts[None, :], q_t.reshape(HEADS, HEAD, tok_rows), kv_all)

    pages_here = tok_rows // PAGE
    pages_block = page_table.shape[1]
    slot_ids = tensor_index * pages_here + jnp.arange(pages_here, dtype=jnp.int32)
    matches = page_table[0][None, :] == slot_ids[:, None]
    logical = jnp.sum(
        jnp.where(matches, jnp.arange(pages_block, dtype=jnp.int32)[None, :], 0), axis=1
    )
    cache_pages = jnp.stack(
        [
            lax.dynamic_slice(
                kv_all,
                (logical[i] // pages_here, (logical[i] % pages_here) * PAGE, 0),
                (1, PAGE, kvw),
            )[0]
            for i in range(pages_here)
        ]
    )

    held, _ = lax.optimization_barrier((w_out, kv))
    out_t = lax.all_gather(held.T, "tensor", axis=0, tiled=True)
    attn_out = lax.dot_general(
        ctx.reshape(query_width, tok_rows), out_t, (((0,), (1,)), ((), ())),
        preferred_element_type=F32,
    )
    residual = (tokens.astype(F32) + attn_out).astype(BF16)
    expert_input = rms_scaled(residual, moe_gain)

    experts_all = w_gate.shape[0] * tensor_size
    capacity = max(2, 3 * tok_rows * TOP // (2 * experts_all))
    flat_routes = route_ids.reshape(-1)
    expert_hits = (
        flat_routes[:, None] == jnp.arange(experts_all, dtype=jnp.int32)[None, :]
    ).astype(jnp.int32)
    earlier_hits = jnp.cumsum(expert_hits, axis=0) - expert_hits
    slot_rank = jnp.sum(earlier_hits * expert_hits, axis=1)
    dest_slot = (flat_routes * capacity + slot_rank).reshape(tok_rows, TOP)
    slot_table = (
        jnp.arange(experts_all * capacity, dtype=jnp.int32)[:, None, None] == dest_slot[None]
    )
    dispatch = jnp.any(slot_table, axis=2).astype(BF16)
    spread = jnp.sum(
        jnp.where(
            jnp.arange(experts_all * capacity, dtype=jnp.int32)[None, :, None]
            == dest_slot[:, None, :],
            route_weight[:, None, :],
            0.0,
        ),
        axis=2,
    )
    high = spread.astype(BF16)
    low = (spread - high.astype(F32)).astype(BF16)
    outgoing = jnp.dot(dispatch, expert_input, preferred_element_type=F32).astype(BF16)
    outgoing = outgoing.reshape(experts_all, capacity, expert_input.shape[1])
    arrived = lax.all_to_all(outgoing, "tensor", split_axis=0, concat_axis=0, tiled=True)
    rows_flat = arrived.reshape(-1, arrived.shape[-1])
    gate_out = jnp.dot(rows_flat, w_gate[0], preferred_element_type=F32)
    up_out = jnp.dot(rows_flat, w_up[0], preferred_element_type=F32)
    hidden = (jnp.maximum(gate_out, 0.0) * up_out).astype(BF16)
    produced = jnp.dot(hidden, w_down[0], preferred_element_type=F32).astype(BF16)
    returned = lax.all_to_all(
        produced.reshape(arrived.shape), "tensor", split_axis=0, concat_axis=0, tiled=True
    ).reshape(rows_flat.shape)
    routed_sum = jnp.dot(high, returned, preferred_element_type=F32) + jnp.dot(
        low, returned, preferred_element_type=F32
    )
    mixed = (residual.astype(F32) + routed_sum).astype(BF16)
    return (mixed, cache_pages)


def solution(mesh):
    return jax.shard_map(
        body,
        mesh=mesh,
        in_specs=(
            P(("seq", "tensor"), None),
            P(("seq", "tensor")),
            P("seq", None),
            P(),
            P(None, "tensor"),
            P(None, "tensor"),
            P(),
            P(("seq", "tensor"), None),
            P(("seq", "tensor"), None),
            P("tensor", None, None),
            P("tensor", None, None),
            P("tensor", None, None),
        ),
        out_specs=(P(("seq", "tensor"), None), P(("seq", "tensor"), None, None)),
        check_vma=False,
    )
```

time: 426 us -> 290 us (0.68)
  waiting for transfers between devices: 212 us -> 126 us
  blocking collectives: 75.1 us -> 36.7 us
  other arithmetic: 44.8 us -> 14 us
  matrix products: 49.4 us -> 29.7 us
  between operations: 14 us -> 33.6 us
  Pallas kernels: 0 us -> 17 us
    ppermute x2 -> x1, waiting for transfers between devices: 62.6 us -> 8.79 us  [body(): lax.ppermute(sent, 'seq', [(i, i + 1) for i in range(seq_size - 1)])]
    sub x2 -> x0, other arithmetic: 27.8 us -> none  [attend(): weights = jnp.exp(scores - highest)]
    all_to_all x1, waiting for transfers between devices: 27.3 us -> 0.01 us  [body(): lax.all_to_all(produced.reshape(arrived.shape), 'tensor', split_axis=0, c...]
    all_gather x1 -> x0, blocking collectives: 20.8 us -> none  [body(): lax.all_gather(segment_ids, 'tensor', axis=0, tiled=True)]
    dot_general x10 -> x8, matrix products: 49.4 us -> 29.7 us  [the longest x1 9.09 us: body(): jnp.dot(hidden, w_down[0], preferred_element_type=F32).astype(BF16)]
    pallas_call x0 -> x1, Pallas kernels: none -> 17 us  [attention(): pl.pallas_call(attention_kernel, out_shape=jax.ShapeDtypeStruct((HEADS, H...]
    all_to_all x1 -> x0, blocking collectives: 16.9 us -> none  [body(): lax.all_to_all(own_columns, 'tensor', split_axis=0, concat_axis=1, tiled=...]
    gather x2 -> x0, local copies, waits for them, and re-layouts: 9.78 us -> none  [the longest x1 6.39 us: body(): returned.reshape(-1, returned.shape[-1])[dest_slot]]
  transfers between devices with their start and end apart: 6 -> 5, of which waited for: 4 -> 4; matrix products, arithmetic and copies ran while one was open for 15% -> 13% of each run, Pallas kernels for 0% -> 6%
where the time goes in v1:
time: 290 us; the launch traced here: 288 us
  waiting for transfers between devices  126 us (43%)
  blocking collectives  36.7 us (13%)
  between operations  33.6 us (12%)
  matrix products  29.7 us (10%)
  local copies, waits for them, and re-layouts  21.5 us (7%)
  Pallas kernels  17 us (6%)
  other arithmetic  14 us (5%)
  starting transfers between devices  9.23 us (3%)
    all_gather x1, waiting for transfers between devices, body(): qkv_t = lax.all_gather(w_qkv.T, 'tensor', axis=0, tiled=True)  43.5 us
    all_gather x1, waiting for transfers between devices, body(): kv_all = lax.all_gather(chunk, 'tensor', axis=0, tiled=False)  38.6 us
    all_to_all x1, blocking collectives, body(): lax.all_to_all(outgoing, 'tensor', split_axis=0, concat_axis=0, tiled=True)  36.7 us
    all_gather x1, waiting for transfers between devices, body(): out_t = lax.all_gather(held.T, 'tensor', axis=0, tiled=True)  33.9 us
    pallas_call x1, Pallas kernels, attention(): pl.pallas_call(attention_kernel, out_shape=jax.ShapeDtypeStruct((HEADS, H...  17 us
    unnamed x32, local copies, waits for them, and re-layouts  12.1 us
    dot_general x1, matrix products, body(): jnp.dot(hidden, w_down[0], preferred_element_type=F32).astype(BF16)  9.09 us
    ppermute x1, waiting for transfers between devices, body(): lax.ppermute(sent, 'seq', [(i, i + 1) for i in range(seq_size - 1)])  8.79 us
  transfers between devices with their start and end apart: 5, of which 4 were waited for; matrix products, arithmetic and copies ran while one was open for 13% of the time, Pallas kernels for 6%

profile of v1, /device:TPU:1, one launch (start us, length us, event | category | flops | bytes accessed | tf_op | source)
XLA Modules:
  0.0 287.9 jit_solution(3666060145110644619)
XLA Ops:
  7.2 0.7 all-gather.5.cloned.1.call-update
  8.0 0.8 convert_reduce_fusion
  8.8 1.0 fusion.33
  9.8 4.4 %collective-permute-start = (bf16[144,1536]{1,0:T(8,128)(2,1)S(1)}, bf16[144,1536]{1,0:T(8,128)(2,1)S(1)}, u32[]{:S(2)}, u32[]{:S(2)}) collective-permute-start(bf16[144,1536]{1,0:T(8,128)(2,1)S(1)} %fusion.33), channel_id=1, source_target_pairs={{0,32},{32,64},{64,96},{96,128},{128,160},{160,192},{192,224},{1,3... | collective-permute-start | bytes 1327112 | tf_op jit(solution)/shard_map/ppermute | solution.py:130
  14.2 8.8 %collective-permute-done = bf16[144,1536]{1,0:T(8,128)(2,1)S(1)} collective-permute-done((bf16[144,1536]{1,0:T(8,128)(2,1)S(1)}, bf16[144,1536]{1,0:T(8,128)(2,1)S(1)}, u32[]{:S(2)}, u32[]{:S(2)}) %collective-permute-start) | collective-permute-done | bytes 442400 | tf_op jit(solution)/shard_map/ppermute | solution.py:130
  23.0 1.2 fusion.19
  24.3 1.1 fusion.21
  25.4 43.5 %all-gather.5.cloned.1.call-done = bf16[2048,1536]{1,0:T(8,128)(2,1)} async-done(((bf16[64,1536]{1,0:T(8,128)(2,1)}), bf16[2048,1536]{1,0:T(8,128)(2,1)}) %all-gather.5.cloned.1.call-update) | async-done | bytes 6291472 | tf_op jit(solution)/shard_map/all_gather | solution.py:133
  69.0 2.3 fusion.25
  71.3 0.7 fusion.38
  72.1 0.7 all-gather.7.cloned.1.call-update
  72.8 1.4 copy.38
  74.2 0.9 eq.100
  75.1 0.9 eq.96
  76.1 0.6 fusion.45
  76.7 3.2 %reduce-window.6 = s32[32,4,128]{2,0,1:T(8,128)} reduce-window(s32[32,4,128]{2,0,1:T(8,128)} %fusion.45, s32[]{:T(128)} %constant.130.clone.1), window={size=1x1x128 pad=0_0x0_0x127_0}, to_apply=%region_4.5 | reduce-window | flops 2080768 | bytes 131076 | tf_op jit(solution)/shard_map/reduce-window
  79.9 1.1 slice_reduce_fusion
  81.0 0.9 fusion.44
  82.0 0.7 reduce_sum.79
  82.7 0.9 copy.41
  83.6 0.7 multiply_add_fusion
  84.3 0.9 fusion.24
  85.2 4.7 %fusion.14 = bf16[1536,128]{0,1:T(8,128)(2,1)} fusion(bf16[2048,1536]{1,0:T(8,128)(2,1)} %all-gather.5.cloned.1.call-done, bf16[256,1536]{1,0:T(8,128)(2,1)S(1)} %copy-done.3), kind=kOutput, calls=%fused_computation.17 | convolution fusion | flops 604176384 | bytes 5505024 | tf_op jit(solution)/shard_map/dot_general | solution.py:135
  89.9 2.0 copy.37
  91.9 38.6 %all-gather.9.cloned.1.call-done = bf16[8704,512]{1,0:T(8,128)(2,1)} async-done(((bf16[272,512]{1,0:T(8,128)(2,1)}), bf16[8704,512]{1,0:T(8,128)(2,1)}) %all-gather.9.cloned.1.call-update) | async-done | bytes 8912912 | tf_op jit(solution)/shard_map/all_gather | solution.py:145
  130.5 0.8 slice.81
  131.3 0.9 broadcast_select_fusion
  132.3 1.3 select_reduce_fusion.1
  133.6 17.0 %window_attention.1 = bf16[12,128,128]{2,1,0:T(8,128)(2,1)} custom-call(s32[1,128]{1,0:T(1,128)} %bitcast.93, bf16[12,128,128]{2,1,0:T(8,128)(2,1)} %bitcast.75, bf16[32,272,512]{2,1,0:T(8,128)(2,1)} %bitcast.81), custom_call_target="tpu_custom_call" | custom-call | flops 3321888768 | bytes 8912896 | tf_op jit(solution)/shard_map/window_attention/pallas_call | solution.py:85
  150.6 33.9 %all-gather.7.cloned.1.call-done = bf16[1536,1536]{1,0:T(8,128)(2,1)} async-done(((bf16[48,1536]{1,0:T(8,128)(2,1)}), bf16[1536,1536]{1,0:T(8,128)(2,1)}) %all-gather.7.cloned.1.call-update) | async-done | bytes 4718608 | tf_op jit(solution)/shard_map/all_gather | solution.py:183
  184.5 4.2 %multiply_reduce_fusion = (f32[128]{0:T(128)S(1)}, f32[128,1536]{1,0:T(8,128)S(1)}) fusion(bf16[1536,128]{1,0:T(8,128)(2,1)} %bitcast.74, bf16[1536,1536]{1,0:T(8,128)(2,1)} %all-gather.7.cloned.1.call-done, bf16[128,1536]{1,0:T(8,128)(2,1)S(1)} %copy-done.1), kind=kOutput, calls=%fused_computation.36 | convolution fusion | flops 605159296 | bytes 6291968 | tf_op jit(solution)/shard_map/dot_general | solution.py:184
  188.8 0.8 convolution_convert_fusion.1
  189.7 36.7 %all_to_all.10 = bf16[32,24,1536]{2,1,0:T(8,128)(2,1)S(1)} all-to-all(bf16[32,24,1536]{2,1,0:T(8,128)(2,1)S(1)} %bitcast.70), channel_id=1, replica_groups=mesh['seq'=8,'tensor'=32] {'tensor'}, dimensions={0} | all-to-all | bytes 4718592 | tf_op jit(solution)/shard_map/all_to_all | solution.py:217
  226.3 1.4 copy-done.2
  227.7 3.5 %fusion.10 = f32[768,768]{1,0:T(8,128)} fusion(bf16[768,1536]{1,0:T(8,128)(2,1)S(1)} %bitcast.72, bf16[1,1536,768]{2,1,0:T(8,128)(2,1)S(1)} %copy-done.11), kind=kOutput, calls=%fused_computation.12 | convolution fusion | flops 1811939328 | bytes 7077888 | tf_op jit(solution)/shard_map/dot_general | solution.py:220
  231.2 9.1 %convolution_convert_fusion = bf16[768,1536]{1,0:T(8,128)(2,1)} fusion(bf16[1,768,1536]{2,1,0:T(8,128)(2,1)S(1)} %copy-done, f32[768,768]{1,0:T(8,128)} %fusion.10, bf16[768,1536]{1,0:T(8,128)(2,1)} %bitcast.73, bf16[1,1536,768]{2,1,0:T(8,128)(2,1)} %param.21), kind=kOutput, calls=%fused_computation.2 | convolution fusion | flops 3626827776 | bytes 11796480 | tf_op jit(solution)/shard_map/dot_general | solution.py:222
  240.3 4.7 %all-to-all-start.1 = ((bf16[32,24,1536]{2,1,0:T(8,128)(2,1)}), bf16[32,24,1536]{2,1,0:T(8,128)(2,1)}, u32[]{:S(2)}, u32[]{:S(2)}) async-start(bf16[32,24,1536]{2,1,0:T(8,128)(2,1)} %bitcast.71), calls=%async_computation.1 | async-start | bytes 4718592 | tf_op jit(solution)/shard_map/all_to_all | solution.py:223
  245.2 0.6 fusion.49
  265.7 1.3 constant_dynamic-update-slice_fusion.7
  267.1 1.3 constant_dynamic-update-slice_fusion.6
  268.4 1.3 constant_dynamic-update-slice_fusion.5
  269.7 1.3 constant_dynamic-update-slice_fusion.4
  271.0 1.3 constant_dynamic-update-slice_fusion.3
  272.4 1.3 constant_dynamic-update-slice_fusion.2
  273.7 1.3 constant_dynamic-update-slice_fusion.1
  275.0 1.3 constant_dynamic-update-slice_fusion
  276.3 2.1 fusion.40
  278.5 2.9 %fusion.3 = bf16[128,1536]{1,0:T(8,128)(2,1)} fusion(f32[128,1536]{1,0:T(8,128)S(1)} %get-tuple-element.13, f32[128,1536]{1,0:T(8,128)S(1)} %fusion.40, bf16[768,1536]{1,0:T(8,128)(2,1)} %bitcast.17, f32[128,768]{1,0:T(8,128)S(1)} %select_reduce_fusion), kind=kOutput, calls=%fused_computation.7 | convolution fusion | flops 302972928 | bytes 4718592 | tf_op jit(solution)/shard_map/dot_general | solution.py:226
  (40 shorter events, 0.8 us)
Async XLA Ops:
  7.2 224.0 %copy-start = (bf16[1,768,1536]{2,1,0:T(8,128)(2,1)S(1)}, bf16[1,768,1536]{2,1,0:T(8,128)(2,1)}, u32[]{:S(2)}) copy-start(bf16[1,768,1536]{2,1,0:T(8,128)(2,1)} %param.23) | copy-start | bytes 7077892
  7.2 17.1 %copy-start.1 = (bf16[128,1536]{1,0:T(8,128)(2,1)S(1)}, bf16[128,1536]{1,0:T(8,128)(2,1)}, u32[]{:S(2)}) copy-start(bf16[128,1536]{1,0:T(8,128)(2,1)} %param.12) | copy-start | bytes 1179652
  7.2 17.1 %copy-start.5 = (f32[1536]{0:T(1024)S(1)}, f32[1536]{0:T(1024)}, u32[]{:S(2)}) copy-start(f32[1536]{0:T(1024)} %param.15) | copy-start | bytes 18436
  7.2 61.8 %all-gather.5.cloned.1.call-start = ((), (), s32[]{:S(2)}) async-start(), calls=%async_computation.2 | async-start | bytes 6488064 | tf_op jit(solution)/shard_map/all_gather | solution.py:133
  7.9 122.5 %all-gather.9.cloned.1.call-start = ((), (), s32[]{:S(2)}) async-start(), calls=%async_computation.4 | async-start | bytes 9191424 | tf_op jit(solution)/shard_map/all_gather | solution.py:145
  8.8 15.5 %copy-start.8 = (bf16[128]{0:T(256)(128)(2,1)}, bf16[128]{0:T(256)(128)(2,1)S(1)}, u32[]{:S(2)}) copy-start(bf16[128]{0:T(256)(128)(2,1)S(1)} %convert_reduce_fusion) | copy-start | bytes 772
  9.8 13.2 %collective-permute-start = (bf16[144,1536]{1,0:T(8,128)(2,1)S(1)}, bf16[144,1536]{1,0:T(8,128)(2,1)S(1)}, u32[]{:S(2)}, u32[]{:S(2)}) collective-permute-start(bf16[144,1536]{1,0:T(8,128)(2,1)S(1)} %fusion.33), channel_id=1, source_target_pairs={{0,32},{32,64},{64,96},{96,128},{128,160},{160,192},{192,224},{1,3... | collective-permute-start | bytes 1327112 | tf_op jit(solution)/shard_map/ppermute | solution.py:130
  25.4 59.7 %copy-start.3 = (bf16[256,1536]{1,0:T(8,128)(2,1)S(1)}, bf16[256,1536]{1,0:T(8,128)(2,1)}, u32[]{:S(2)}) copy-start(bf16[256,1536]{1,0:T(8,128)(2,1)} %fusion.21) | copy-start | bytes 2359300
  69.0 2.3 copy-start.9
  72.0 112.5 %all-gather.7.cloned.1.call-start = ((), (), s32[]{:S(2)}) async-start(), calls=%async_computation.3 | async-start | bytes 4866048 | tf_op jit(solution)/shard_map/all_gather | solution.py:183
  184.5 4.2 %copy-start.4 = (pred[768,128]{1,0:T(8,128)(4,1)S(1)}, pred[768,128]{1,0:T(8,128)(4,1)}, u32[]{:S(2)}) copy-start(pred[768,128]{1,0:T(8,128)(4,1)} %fusion.24) | copy-start | bytes 294916
  184.5 4.3 %copy-start.6 = (f32[1536]{0:T(1024)S(1)}, f32[1536]{0:T(1024)}, u32[]{:S(2)}) copy-start(f32[1536]{0:T(1024)} %param.18) | copy-start | bytes 18436
  189.6 38.1 %copy-start.11 = (bf16[1,1536,768]{2,1,0:T(8,128)(2,1)S(1)}, bf16[1,1536,768]{2,1,0:T(8,128)(2,1)}, u32[]{:S(2)}) copy-start(bf16[1,1536,768]{2,1,0:T(8,128)(2,1)} %param.22) | copy-start | bytes 7077892
  226.3 1.4 copy-start.2
  240.3 4.7 %copy-start.10 = (s32[1,256]{1,0:T(1,128)S(1)}, s32[1,256]{1,0:T(1,128)}, u32[]{:S(2)}) copy-start(s32[1,256]{1,0:T(1,128)} %param.14) | copy-start | bytes 3076
  240.3 25.2 %copy-start.7 = (f32[128,4]{0,1:T(4,128)S(1)}, f32[128,4]{0,1:T(4,128)}, u32[]{:S(2)}) copy-start(f32[128,4]{0,1:T(4,128)} %param.20) | copy-start | bytes 6148
  240.3 36.0 %all-to-all-start.1 = ((bf16[32,24,1536]{2,1,0:T(8,128)(2,1)}), bf16[32,24,1536]{2,1,0:T(8,128)(2,1)}, u32[]{:S(2)}, u32[]{:S(2)}) async-start(bf16[32,24,1536]{2,1,0:T(8,128)(2,1)} %bitcast.71), calls=%async_computation.1 | async-start | bytes 4718592 | tf_op jit(solution)/shard_map/all_to_all | solution.py:223
Sparse Core Ops, SparseCore 0:
  10.6 58.3 all-gather.4
  72.1 58.2 all-gather.8
  133.0 51.4 all-gather.6

commit v2 on v1

--- a/solution.py
+++ b/solution.py
@@ -80,6 +80,177 @@
         out_ref[head] = (acc[head] / total[head : head + 1, :]).astype(BF16)
 
 
+RING = 4
+FULL_A, HALF_A, FULL_B, HALF_B, PAIR = 0, 2, 4, 12, 20
+COPIES = 36
+ORDER = (0, -1, 1, 2)
+
+
+def gather_kernel(splits, with_seq, *refs):
+    count = len(splits)
+    refs = list(refs)
+    shards = refs[:count]
+    refs = refs[count:]
+    if with_seq:
+        sent_ref = refs.pop(0)
+    outs = refs[:count]
+    refs = refs[count:]
+    if with_seq:
+        got_ref = refs.pop(0)
+    send, recv, here = refs[:3]
+    place = lax.axis_index("tensor")
+    core = lax.rem(place, 2)
+    px = lax.rem(place // 2, RING)
+    py = place // (2 * RING)
+
+    def at(a, b, flip=0):
+        x = lax.rem(px + a * (1 - core) + b * core + RING, RING)
+        y = lax.rem(py + a * core + b * (1 - core) + RING, RING)
+        c = (1 - core) if flip else core
+        return (y * RING + x) * 2 + c
+
+    barrier = pltpu.get_barrier_semaphore()
+    peers = [at(1, 0), at(-1, 0), at(0, 1), at(0, -1), at(0, 0, 1)]
+    for peer in peers:
+        pl.semaphore_signal(
+            barrier, inc=1, device_id={"tensor": peer}, device_id_type=pl.DeviceIdType.MESH
+        )
+    if with_seq:
+        seq = lax.axis_index("seq")
+        seq_size = lax.axis_size("seq")
+        later = lax.rem(seq + 1, seq_size)
+        for peer in (later, lax.rem(seq + seq_size - 1, seq_size)):
+            pl.semaphore_signal(
+                barrier, inc=1, device_id={"seq": peer}, device_id_type=pl.DeviceIdType.MESH
+            )
+    pl.semaphore_wait(barrier, 7 if with_seq else 5)
+
+    def view(n, a, b, part):
+        ref = outs[n].at[at(a, b)]
+        if part is None:
+            return ref
+        axis, cut = splits[n]
+        rows, cols = outs[n].shape[1:]
+        whole = rows if axis == 0 else cols
+        span = pl.ds(0, cut) if part == 0 else pl.ds(cut, whole - cut)
+        return ref.at[span, :] if axis == 0 else ref.at[:, span]
+
+    def copy(n, kind, a, b, part, target):
+        src = shards[n] if (a == 0 and b == 0) else view(n, a, b, part)
+        return pltpu.make_async_remote_copy(
+            src_ref=src,
+            dst_ref=view(n, a, b, part),
+            send_sem=send.at[n, kind],
+            recv_sem=recv.at[n, kind],
+            device_id={"tensor": target},
+            device_id_type=pl.DeviceIdType.MESH,
+        )
+
+    started = []
+
+    def go(n, kind, a, b, part, target):
+        c = copy(n, kind, a, b, part, target)
+        c.start()
+        started.append(c)
+
+    def landed(n, kind, a, b, part):
+        copy(n, kind, a, b, part, at(0, 0, 1)).wait_recv()
+
+    def spread(n, k):
+        r = ORDER[k]
+        go(n, FULL_B + 2 * k, r, 0, None, at(0, 1))
+        go(n, FULL_B + 2 * k + 1, r, 0, None, at(0, -1))
+        go(n, PAIR + k, r, 0, None, at(0, 0, 1))
+
+    own = []
+    for n in range(count):
+        go(n, FULL_A, 0, 0, None, at(1, 0))
+        go(n, FULL_A + 1, 0, 0, None, at(-1, 0))
+        spread(n, 0)
+    for n in range(count):
+        c = pltpu.make_async_copy(shards[n], outs[n].at[place], here.at[n])
+        c.start()
+        own.append(c)
+    if with_seq:
+        z = pltpu.make_async_remote_copy(
+            src_ref=sent_ref,
+            dst_ref=got_ref,
+            send_sem=here.at[count],
+            recv_sem=here.at[count + 1],
+            device_id={"seq": later},
+            device_id_type=pl.DeviceIdType.MESH,
+        )
+        z.start()
+    for n in range(count):
+        landed(n, FULL_A, -1, 0, None)
+        go(n, HALF_A, -1, 0, 0, at(1, 0))
+        spread(n, 1)
+        landed(n, FULL_A + 1, 1, 0, None)
+        go(n, HALF_A + 1, 1, 0, 1, at(-1, 0))
+        spread(n, 2)
+    for n in range(count):
+        for k in (0, 1, 2, 3):
+            r = ORDER[k]
+            if k == 1:
+                landed(n, HALF_A, 2, 0, 0)
+                landed(n, HALF_A + 1, 2, 0, 1)
+                spread(n, 3)
+            landed(n, FULL_B + 2 * k, r, -1, None)
+            go(n, HALF_B + 2 * k, r, -1, 0, at(0, 1))
+            go(n, PAIR + 4 + k, r, -1, None, at(0, 0, 1))
+            landed(n, FULL_B + 2 * k + 1, r, 1, None)
+            go(n, HALF_B + 2 * k + 1, r, 1, 1, at(0, -1))
+            go(n, PAIR + 8 + k, r, 1, None, at(0, 0, 1))
+    for n in range(count):
+        for k in range(RING):
+            landed(n, HALF_B + 2 * k, ORDER[k], 2, 0)
+            landed(n, HALF_B + 2 * k + 1, ORDER[k], 2, 1)
+            go(n, PAIR + 12 + k, ORDER[k], 2, None, at(0, 0, 1))
+    for c in own:
+        c.wait()
+    if with_seq:
+        z.wait()
+    for n in range(count):
+        for k in range(4 * RING):
+            pltpu.make_async_remote_copy(
+                src_ref=outs[n].at[place],
+                dst_ref=outs[n].at[place],
+                send_sem=send.at[n, PAIR + k],
+                recv_sem=recv.at[n, PAIR + k],
+                device_id={"tensor": at(0, 0, 1)},
+                device_id_type=pl.DeviceIdType.MESH,
+            ).wait_recv()
+    for c in started:
+        c.wait_send()
+
+
+def gather(shards, splits, number, sent=None):
+    places = lax.axis_size("tensor")
+    vm = pl.BlockSpec(memory_space=pltpu.VMEM)
+    anyspace = pl.BlockSpec(memory_space=pl.ANY)
+    with_seq = sent is not None
+    out_shape = [jax.ShapeDtypeStruct((places,) + s.shape, s.dtype) for s in shards]
+    args = list(shards)
+    out_specs = [anyspace] * len(shards)
+    if with_seq:
+        args.append(sent)
+        out_shape.append(jax.ShapeDtypeStruct(sent.shape, sent.dtype))
+        out_specs.append(vm)
+    return pl.pallas_call(
+        functools.partial(gather_kernel, splits, with_seq),
+        out_shape=out_shape,
+        in_specs=[vm] * len(args),
+        out_specs=out_specs,
+        scratch_shapes=[
+            pltpu.SemaphoreType.DMA((len(shards), COPIES)),
+            pltpu.SemaphoreType.DMA((len(shards), COPIES)),
+            pltpu.SemaphoreType.DMA((len(shards) + 2,)),
+        ],
+        compiler_params=pltpu.CompilerParams(collective_id=number, has_side_effects=True),
+        name="gather_%d" % number,
+    )(*args)
+
+
 def attention(starts, q_t, kv_all):
     vm = pl.BlockSpec(memory_space=pltpu.VMEM)
     return pl.pallas_call(
@@ -119,7 +290,6 @@
     tensor_size = lax.axis_size("tensor")
     tensor_index = lax.axis_index("tensor")
     seq_index = lax.axis_index("seq")
-    seq_size = lax.axis_size("seq")
     query_width = HEADS * HEAD
 
     counts = jnp.sum(
@@ -127,10 +297,10 @@
     ).astype(BF16)
     counts_rows = jnp.pad(counts[None, :], ((0, PAGE - 1), (0, tokens.shape[1] - TOK)))
     sent = jnp.concatenate([tokens, counts_rows], axis=0)
-    earlier = lax.ppermute(sent, "seq", [(i, i + 1) for i in range(seq_size - 1)])
+    qkv_t, earlier = gather([w_qkv.T], [(0, w_qkv.shape[1] // 2)], 0, sent)
+    qkv_t = qkv_t.reshape(-1, tokens.shape[1])
     both = jnp.concatenate([tokens, earlier[:tok_rows]], axis=0)
     normed = rms_scaled(both, attn_gain)
-    qkv_t = lax.all_gather(w_qkv.T, "tensor", axis=0, tiled=True)
     nt = (((1,), (1,)), ((), ()))
     q_t = lax.dot_general(
         qkv_t[:query_width], normed[:tok_rows], nt, preferred_element_type=F32
@@ -142,7 +312,10 @@
          jnp.pad(earlier[tok_rows:, :kvw], ((0, 0), (0, 0)))[: PAGE - 1]], axis=0
     )
     chunk = jnp.concatenate([kv, seg_rows], axis=0)
-    kv_all = lax.all_gather(chunk, "tensor", axis=0, tiled=False)
+    kv_all, out_t = gather(
+        [chunk, w_out.T], [(0, tok_rows + PAGE), (1, query_width // 2)], 1
+    )
+    out_t = out_t.reshape(-1, query_width)
 
     own_counts = kv_all[:, 2 * tok_rows, :TOK].astype(F32)
     prev_counts = kv_all[:, 2 * tok_rows + 1, :TOK].astype(F32)
@@ -179,8 +352,6 @@
         ]
     )
 
-    held, _ = lax.optimization_barrier((w_out, kv))
-    out_t = lax.all_gather(held.T, "tensor", axis=0, tiled=True)
     attn_out = lax.dot_general(
         ctx.reshape(query_width, tok_rows), out_t, (((0,), (1,)), ((), ())),
         preferred_element_type=F32,
@@ -190,26 +361,16 @@
 
     experts_all = w_gate.shape[0] * tensor_size
     capacity = max(2, 3 * tok_rows * TOP // (2 * experts_all))
-    flat_routes = route_ids.reshape(-1)
-    expert_hits = (
-        flat_routes[:, None] == jnp.arange(experts_all, dtype=jnp.int32)[None, :]
-    ).astype(jnp.int32)
-    earlier_hits = jnp.cumsum(expert_hits, axis=0) - expert_hits
-    slot_rank = jnp.sum(earlier_hits * expert_hits, axis=1)
-    dest_slot = (flat_routes * capacity + slot_rank).reshape(tok_rows, TOP)
-    slot_table = (
-        jnp.arange(experts_all * capacity, dtype=jnp.int32)[:, None, None] == dest_slot[None]
-    )
-    dispatch = jnp.any(slot_table, axis=2).astype(BF16)
-    spread = jnp.sum(
-        jnp.where(
-            jnp.arange(experts_all * capacity, dtype=jnp.int32)[None, :, None]
-            == dest_slot[:, None, :],
-            route_weight[:, None, :],
-            0.0,
-        ),
-        axis=2,
-    )
+    picks = route_ids.T[None] == jnp.arange(experts_all, dtype=jnp.int32)[:, None, None]
+    hits = jnp.any(picks, axis=1)
+    weights = jnp.sum(jnp.where(picks, route_weight.T[None], 0.0), axis=1)
+    order_of = jnp.arange(tok_rows, dtype=jnp.int32)
+    ahead = (order_of[:, None] < order_of[None, :]).astype(BF16)
+    ranks = jnp.dot(hits.astype(BF16), ahead, preferred_element_type=F32)
+    slots = jnp.arange(capacity, dtype=jnp.int32).astype(F32)[None, :, None]
+    taken = jnp.logical_and(hits[:, None, :], ranks[:, None, :] == slots)
+    dispatch = taken.astype(BF16).reshape(experts_all * capacity, tok_rows)
+    spread = jnp.where(taken, weights[:, None, :], 0.0).reshape(experts_all * capacity, tok_rows)
     high = spread.astype(BF16)
     low = (spread - high.astype(F32)).astype(BF16)
     outgoing = jnp.dot(dispatch, expert_input, preferred_element_type=F32).astype(BF16)
@@ -223,9 +384,10 @@
     returned = lax.all_to_all(
         produced.reshape(arrived.shape), "tensor", split_axis=0, concat_axis=0, tiled=True
     ).reshape(rows_flat.shape)
-    routed_sum = jnp.dot(high, returned, preferred_element_type=F32) + jnp.dot(
-        low, returned, preferred_element_type=F32
-    )
+    tn = (((0,), (0,)), ((), ()))
+    routed_sum = lax.dot_general(
+        high, returned, tn, preferred_element_type=F32
+    ) + lax.dot_general(low, returned, tn, preferred_element_type=F32)
     mixed = (residual.astype(F32) + routed_sum).astype(BF16)
     return (mixed, cache_pages)
 

time: 290 us -> 230 us (0.79)
  waiting for transfers between devices: 126 us -> 4.45 us
  Pallas kernels: 17 us -> 96.8 us
  between operations: 33.6 us -> 21 us
  local copies, waits for them, and re-layouts: 21.5 us -> 30.6 us
  other arithmetic: 14 us -> 6.68 us
  starting transfers between devices: 9.23 us -> 4.74 us
    all_gather x3 -> x0, waiting for transfers between devices: 116 us -> none  [the longest x1 43.5 us: body(): qkv_t = lax.all_gather(w_qkv.T, 'tensor', axis=0, tiled=True)]
    pallas_call x0 -> x2, Pallas kernels: none -> 79.6 us  [gather(): pl.pallas_call(functools.partial(gather_kernel, splits, with_seq), out_sh...]
    pallas_call x0 -> x1, local copies, waits for them, and re-layouts: none -> 12 us  [gather(): pl.pallas_call(functools.partial(gather_kernel, splits, with_seq), out_sh...]
    ppermute x1 -> x0, waiting for transfers between devices: 8.79 us -> none  [body(): lax.ppermute(sent, 'seq', [(i, i + 1) for i in range(seq_size - 1)])]
    slice x2, local copies, waits for them, and re-layouts: 1.9 us -> 7.71 us  [the longest x1 5.06 us: body(): qkv_t[:query_width]]
    unnamed x32 -> x45, local copies, waits for them, and re-layouts: 12.1 us -> 7.09 us
    all_to_all x1, waiting for transfers between devices: 0.01 us -> 4.45 us  [body(): lax.all_to_all(produced.reshape(arrived.shape), 'tensor', split_axis=0, c...]
    ppermute x1 -> x0, starting transfers between devices: 4.4 us -> none  [body(): lax.ppermute(sent, 'seq', [(i, i + 1) for i in range(seq_size - 1)])]
  transfers between devices with their start and end apart: 5 -> 1, of which waited for: 4 -> 1; matrix products, arithmetic and copies ran while one was open for 13% -> 3% of each run, Pallas kernels for 6% -> 0%
where the time goes in v2:
time: 230 us; the launch traced here: 229 us
  Pallas kernels  96.8 us (42%)
  blocking collectives  36.3 us (16%)
  local copies, waits for them, and re-layouts  30.6 us (13%)
  matrix products  28.2 us (12%)
  between operations  21 us (9%)
  other arithmetic  6.68 us (3%)
  starting transfers between devices  4.74 us (2%)
  waiting for transfers between devices  4.45 us (2%)
    pallas_call x2, Pallas kernels, gather(): pl.pallas_call(functools.partial(gather_kernel, splits, with_seq), out_sh...  79.6 us
    all_to_all x1, blocking collectives, body(): lax.all_to_all(outgoing, 'tensor', split_axis=0, concat_axis=0, tiled=True)  36.3 us
    pallas_call x1, Pallas kernels, attention(): pl.pallas_call(attention_kernel, out_shape=jax.ShapeDtypeStruct((HEADS, H...  17.2 us
    pallas_call x1, local copies, waits for them, and re-layouts, gather(): pl.pallas_call(functools.partial(gather_kernel, splits, with_seq), out_sh...  12 us
    dot_general x1, matrix products, body(): jnp.dot(hidden, w_down[0], preferred_element_type=F32).astype(BF16)  9.16 us
    unnamed x45, local copies, waits for them, and re-layouts  7.09 us
    slice x1, local copies, waits for them, and re-layouts, body(): qkv_t[:query_width]  5.06 us
    all_to_all x1, starting transfers between devices, body(): lax.all_to_all(produced.reshape(arrived.shape), 'tensor', split_axis=0, c...  4.74 us
  transfers between devices with their start and end apart: 1, of which 1 were waited for; matrix products, arithmetic and copies ran while one was open for 3% of the time, Pallas kernels for 0%

profile of v2, /device:TPU:1, one launch (start us, length us, event | category | flops | bytes accessed | tf_op | source)
XLA Modules:
  0.0 228.9 jit_solution(3362408374993315718)
XLA Ops:
  0.6 0.0 copy-start
  0.7 0.0 copy-start.12
  0.7 0.9 convert_reduce_fusion
  1.6 1.8 fusion.20.refs_1_
  3.4 34.8 %gather_0.1 = (bf16[32,64,1536]{2,1,0:T(8,128)(2,1)}, bf16[144,1536]{1,0:T(8,128)(2,1)}) custom-call(bf16[64,1536]{1,0:T(8,128)(2,1)} %bitcast.79, bf16[144,1536]{1,0:T(8,128)(2,1)} %fusion.20.refs_1_), custom_call_target="tpu_custom_call" | custom-call | tf_op jit(solution)/shard_map/gather_0/pallas_call | solution.py:239
  38.1 0.7 slice.64
  38.9 1.0 slice.61
  39.9 2.6 %slice.62 = bf16[8,64,1536]{2,1,0:T(8,128)(2,1)} slice(bf16[32,64,1536]{2,1,0:T(8,128)(2,1)} %get-tuple-element.7), slice={[24:32], [0:64], [0:1536]} | slice | bytes 3145728 | tf_op jit(solution)/shard_map/slice | solution.py:308
  42.5 5.1 %slice.67 = bf16[24,64,1536]{2,1,0:T(8,128)(2,1)} slice(bf16[32,64,1536]{2,1,0:T(8,128)(2,1)} %get-tuple-element.7), slice={[0:24], [0:64], [0:1536]} | slice | bytes 9437184 | tf_op jit(solution)/shard_map/slice | solution.py:306
  47.6 0.0 copy-done.10
  47.6 0.6 copy-done.4
  48.2 0.1 fusion.40
  48.4 0.7 eq.95
  49.0 0.2 fusion.12
  49.3 0.2 fusion.14
  49.5 0.0 copy-start.3
  49.6 4.6 %convolution_convert_fusion.2 = bf16[1536,128]{1,0:T(8,128)(2,1)} fusion(bf16[1536,1536]{1,0:T(8,128)(2,1)} %bitcast.72, bf16[256,1536]{1,0:T(8,128)(2,1)S(1)} %fusion.14), kind=kOutput, calls=%fused_computation.8 | convolution fusion | flops 604176384 | bytes 5505024 | tf_op jit(solution)/shard_map/dot_general | solution.py:305
  54.1 0.6 convolution_convert_fusion.3
  54.8 0.7 fusion.27.refs_0_
  55.5 44.9 %gather_1.1 = (bf16[32,272,512]{2,1,0:T(8,128)(2,1)}, bf16[32,48,1536]{2,1,0:T(8,128)(2,1)}) custom-call(bf16[272,512]{1,0:T(8,128)(2,1)} %fusion.27.refs_0_, bf16[48,1536]{1,0:T(8,128)(2,1)} %bitcast.80), custom_call_target="tpu_custom_call" | custom-call | tf_op jit(solution)/shard_map/gather_1/pallas_call | solution.py:239
  100.4 0.0 copy-start.18
  100.4 12.0 %copy.21 = bf16[32,272,512]{2,0,1:T(8,128)(2,1)} copy(bf16[32,272,512]{2,1,0:T(8,128)(2,1)} %get-tuple-element.8.kv_ref) | data formatting | bytes 17825792 | tf_op jit(solution)/shard_map/gather_1/pallas_call | solution.py:239
  112.4 0.9 broadcast_select_fusion
  113.3 0.8 fusion.42
  114.1 0.7 select_reduce_fusion.1
  114.8 17.2 %window_attention.1 = bf16[12,128,128]{2,1,0:T(8,128)(2,1)} custom-call(s32[1,128]{1,0:T(1,128)} %bitcast.89, bf16[12,128,128]{2,1,0:T(8,128)(2,1)} %bitcast.88, bf16[32,272,512]{2,1,0:T(8,128)(2,1)} %get-tuple-element.8.kv_ref), custom_call_target="tpu_custom_call" | custom-call | flops 3321888768 | bytes 8912896 | tf_op jit(solution)/shard_map/window_attention/pallas_call | solution.py:256
  132.0 4.2 %multiply_reduce_fusion = (f32[128]{0:T(128)S(1)}, f32[128,1536]{1,0:T(8,128)S(1)}) fusion(bf16[1536,128]{1,0:T(8,128)(2,1)} %bitcast.78, bf16[1536,1536]{1,0:T(8,128)(2,1)} %bitcast.73, bf16[128,1536]{1,0:T(8,128)(2,1)S(1)} %copy-done.1), kind=kOutput, calls=%fused_computation.29 | convolution fusion | flops 605159296 | bytes 6291968 | tf_op jit(solution)/shard_map/dot_general | solution.py:355
  136.2 0.2 fusion.25
  136.4 0.8 convolution_convert_fusion.1
  137.3 0.0 copy-start.17
  137.3 36.3 %all_to_all.10 = bf16[32,24,1536]{2,1,0:T(8,128)(2,1)S(1)} all-to-all(bf16[32,24,1536]{2,1,0:T(8,128)(2,1)S(1)} %bitcast.71), channel_id=1, replica_groups=mesh['seq'=8,'tensor'=32] {'tensor'}, dimensions={0} | all-to-all | bytes 4718592 | tf_op jit(solution)/shard_map/all_to_all | solution.py:378
  173.7 1.4 copy-done.2
  175.0 3.5 %fusion.6 = f32[768,768]{1,0:T(8,128)} fusion(bf16[768,1536]{1,0:T(8,128)(2,1)S(1)} %bitcast.75, bf16[1,1536,768]{2,1,0:T(8,128)(2,1)S(1)} %copy-done.17), kind=kOutput, calls=%fused_computation.12 | convolution fusion | flops 1811939328 | bytes 7077888 | tf_op jit(solution)/shard_map/dot_general | solution.py:381
  178.5 9.2 %convolution_convert_fusion = bf16[768,1536]{1,0:T(8,128)(2,1)} fusion(bf16[1,768,1536]{2,1,0:T(8,128)(2,1)S(1)} %copy-done, f32[768,768]{1,0:T(8,128)} %fusion.6, bf16[768,1536]{1,0:T(8,128)(2,1)} %bitcast.76, bf16[1,1536,768]{2,1,0:T(8,128)(2,1)} %param.21), kind=kOutput, calls=%fused_computation | convolution fusion | flops 3626827776 | bytes 11796480 | tf_op jit(solution)/shard_map/dot_general | solution.py:383
  187.7 4.7 %all-to-all-start.1 = ((bf16[32,24,1536]{2,1,0:T(8,128)(2,1)}), bf16[32,24,1536]{2,1,0:T(8,128)(2,1)}, u32[]{:S(2)}, u32[]{:S(2)}) async-start(bf16[32,24,1536]{2,1,0:T(8,128)(2,1)} %bitcast.74), calls=%async_computation.1 | async-start | bytes 4718592 | tf_op jit(solution)/shard_map/all_to_all | solution.py:384
  192.4 0.2 select_reduce_fusion.2
  192.6 0.7 fusion.46
  213.4 0.7 constant_dynamic-update-slice_fusion.7
  214.1 0.7 constant_dynamic-update-slice_fusion.6
  214.9 0.7 constant_dynamic-update-slice_fusion.5
  215.6 0.7 constant_dynamic-update-slice_fusion.4
  216.3 0.7 constant_dynamic-update-slice_fusion.3
  217.0 0.7 constant_dynamic-update-slice_fusion.2
  217.7 0.7 constant_dynamic-update-slice_fusion.1
  218.5 0.7 constant_dynamic-update-slice_fusion
  219.2 4.5 %all-to-all-done.1 = bf16[32,24,1536]{2,1,0:T(8,128)(2,1)} async-done(((bf16[32,24,1536]{2,1,0:T(8,128)(2,1)}), bf16[32,24,1536]{2,1,0:T(8,128)(2,1)}, u32[]{:S(2)}, u32[]{:S(2)}) %all-to-all-start.1) | async-done | bytes 2359328 | tf_op jit(solution)/shard_map/all_to_all | solution.py:384
  223.7 2.2 convolution_bitcast_fusion
  225.9 3.0 %fusion.2 = bf16[128,1536]{1,0:T(8,128)(2,1)} fusion(f32[128,1536]{1,0:T(8,128)S(1)} %get-tuple-element.19, f32[128,1536]{1,0:T(8,128)S(1)} %convolution_bitcast_fusion, bf16[32,24,1536]{2,1,0:T(8,128)(2,1)} %all-to-all-done.1, f32[32,128]{1,0:T(8,128)S(1)} %select_reduce_fusion, f32[32,128]{1,0:T(8,128)S(1)} %fusion.40, f32[24]{0:T(128)S(1)} %copy-done.13, ...), kind=kOutput, calls=%fused_computation.7 | convolution fusion | flops 302874624 | bytes 4362336 | tf_op jit(solution)/shard_map/dot_general | solution.py:388
  (39 shorter events, 0.1 us)
Async XLA Ops:
  0.6 177.9 %copy-start = (bf16[1,768,1536]{2,1,0:T(8,128)(2,1)S(1)}, bf16[1,768,1536]{2,1,0:T(8,128)(2,1)}, u32[]{:S(2)}) copy-start(bf16[1,768,1536]{2,1,0:T(8,128)(2,1)} %param.23) | copy-start | bytes 7077892
  0.7 47.7 %copy-start.12 = (f32[24]{0:T(128)}, f32[24]{0:T(128)S(1)}, u32[]{:S(2)}) copy-start(f32[24]{0:T(128)S(1)} %iota_convert_fusion) | copy-start | bytes 292
  42.5 5.1 %copy-start.10 = (s32[128,4]{0,1:T(4,128)S(1)}, s32[128,4]{0,1:T(4,128)}, u32[]{:S(2)}) copy-start(s32[128,4]{0,1:T(4,128)} %param.19) | copy-start | bytes 6148
  42.5 6.5 %copy-start.1 = (bf16[128,1536]{1,0:T(8,128)(2,1)S(1)}, bf16[128,1536]{1,0:T(8,128)(2,1)}, u32[]{:S(2)}) copy-start(bf16[128,1536]{1,0:T(8,128)(2,1)} %param.12) | copy-start | bytes 1179652
  42.5 6.8 %copy-start.8 = (f32[1536]{0:T(1024)S(1)}, f32[1536]{0:T(1024)}, u32[]{:S(2)}) copy-start(f32[1536]{0:T(1024)} %param.15) | copy-start | bytes 18436
  47.6 0.6 copy-start.4
  49.5 4.6 %copy-start.3 = (bf16[8,64,1536]{2,1,0:T(8,128)(2,1)S(1)}, bf16[8,64,1536]{2,1,0:T(8,128)(2,1)}, u32[]{:S(2)}) copy-start(bf16[8,64,1536]{2,1,0:T(8,128)(2,1)} %slice.62) | copy-start | bytes 4718596
  100.4 13.7 %copy-start.18 = (s32[128]{0:T(128)S(1)}, s32[128]{0:T(128)}, u32[]{:S(2)}) copy-start(s32[128]{0:T(128)} %param.13) | copy-start | bytes 1540
  132.0 4.2 %copy-start.5 = (pred[32,128]{1,0:T(8,128)(4,1)S(1)}, pred[32,128]{1,0:T(8,128)(4,1)}, u32[]{:S(2)}) copy-start(pred[32,128]{1,0:T(8,128)(4,1)} %copy-done.4) | copy-start | bytes 12292
  132.0 4.3 %copy-start.7 = (f32[768]{0:T(1024)S(1)}, f32[768]{0:T(1024)}, u32[]{:S(2)}) copy-start(f32[768]{0:T(1024)} %eq.95) | copy-start | bytes 9220
  132.0 4.4 %copy-start.9 = (f32[1536]{0:T(1024)S(1)}, f32[1536]{0:T(1024)}, u32[]{:S(2)}) copy-start(f32[1536]{0:T(1024)} %param.18) | copy-start | bytes 18436
  137.3 37.8 %copy-start.17 = (bf16[1,1536,768]{2,1,0:T(8,128)(2,1)S(1)}, bf16[1,1536,768]{2,1,0:T(8,128)(2,1)}, u32[]{:S(2)}) copy-start(bf16[1,1536,768]{2,1,0:T(8,128)(2,1)} %param.22) | copy-start | bytes 7077892
  173.6 1.4 copy-start.2
  187.7 4.8 %copy-start.16 = (s32[1,256]{1,0:T(1,128)S(1)}, s32[1,256]{1,0:T(1,128)}, u32[]{:S(2)}) copy-start(s32[1,256]{1,0:T(1,128)} %param.14) | copy-start | bytes 3076
  187.7 31.5 %copy-start.11 = (s32[128,4]{0,1:T(4,128)S(1)}, s32[128,4]{0,1:T(4,128)}, u32[]{:S(2)}) copy-start(s32[128,4]{0,1:T(4,128)} %param.19) | copy-start | bytes 6148
  187.7 31.5 %copy-start.14 = (f32[128,4]{0,1:T(4,128)S(1)}, f32[128,4]{0,1:T(4,128)}, u32[]{:S(2)}) copy-start(f32[128,4]{0,1:T(4,128)} %param.20) | copy-start | bytes 6148
  187.7 36.0 %copy-start.6 = (pred[32,128]{1,0:T(8,128)(4,1)S(1)}, pred[32,128]{1,0:T(8,128)(4,1)}, u32[]{:S(2)}) copy-start(pred[32,128]{1,0:T(8,128)(4,1)} %copy-done.4) | copy-start | bytes 12292
  187.7 36.0 %copy-start.13 = (f32[24]{0:T(128)S(1)}, f32[24]{0:T(128)}, u32[]{:S(2)}) copy-start(f32[24]{0:T(128)} %copy-done.12) | copy-start | bytes 292
  187.7 36.0 %all-to-all-start.1 = ((bf16[32,24,1536]{2,1,0:T(8,128)(2,1)}), bf16[32,24,1536]{2,1,0:T(8,128)(2,1)}, u32[]{:S(2)}, u32[]{:S(2)}) async-start(bf16[32,24,1536]{2,1,0:T(8,128)(2,1)} %bitcast.74), calls=%async_computation.1 | async-start | bytes 4718592 | tf_op jit(solution)/shard_map/all_to_all | solution.py:384
  219.2 9.7 %copy-start.15 = (bf16[8,16,512]{2,1,0:T(8,128)(2,1)}, bf16[8,16,512]{2,1,0:T(8,128)(2,1)S(1)}, u32[]{:S(2)}) copy-start(bf16[8,16,512]{2,1,0:T(8,128)(2,1)S(1)} %constant_dynamic-update-slice_fusion) | copy-start | bytes 393220

commit v3 on v1

v3 whole, which is shorter than its diff:
```python
import functools
import math

import jax
import jax.numpy as jnp
from jax import lax
from jax.experimental import pallas as pl
from jax.experimental.pallas import tpu as pltpu
from jax.sharding import PartitionSpec as P

HEADS = 12
KV_HEADS = 2
HEAD = 128
TOP = 4
PAGE = 16
SEGS = 32
CHUNKS = 32
TOK = 128
STEP = 3
NEG = -1e30

epsilon = 1e-06
F32 = jnp.float32
BF16 = jnp.bfloat16


def rms_scaled(values, scales):
    wide = values.astype(F32)
    mean_sq = jnp.mean(wide * wide, axis=-1, keepdims=True)
    return (wide * lax.rsqrt(mean_sq + epsilon) * scales).astype(BF16)


RING = 4
FULL_A, HALF_A, FULL_B, HALF_B, PAIR = 0, 2, 4, 12, 20
COPIES = 36
ORDER = (0, -1, 1, 2)
MESH = pl.DeviceIdType.MESH


class Rings:
    def __init__(self, shards, outs, splits, send, recv, here):
        self.shards, self.outs, self.splits = shards, outs, splits
        self.send, self.recv, self.here = send, recv, here
        self.place = lax.axis_index("tensor")
        self.core = lax.rem(self.place, 2)
        self.px = lax.rem(self.place // 2, RING)
        self.py = self.place // (2 * RING)
        self.started = []
        self.every = range(len(shards))

    def at(self, a, b, flip=0):
        core = self.core
        x = lax.rem(self.px + a * (1 - core) + b * core + RING, RING)
        y = lax.rem(self.py + a * core + b * (1 - core) + RING, RING)
        return (y * RING + x) * 2 + ((1 - core) if flip else core)

    def greet(self, barrier):
        for where in ((1, 0), (-1, 0), (0, 1), (0, -1), (0, 0, 1)):
            pl.semaphore_signal(
                barrier, inc=1, device_id={"tensor": self.at(*where)}, device_id_type=MESH
            )
        return 5

    def view(self, n, a, b, part):
        ref = self.outs[n].at[self.at(a, b)]
        if part is None:
            return ref
        axis, cut = self.splits[n]
        whole = self.outs[n].shape[1 + axis]
        span = pl.ds(0, cut) if part == 0 else pl.ds(cut, whole - cut)
        return ref.at[span, :] if axis == 0 else ref.at[:, span]

    def copy(self, n, kind, a, b, part, where):
        src = self.shards[n] if (a == 0 and b == 0) else self.view(n, a, b, part)
        return pltpu.make_async_remote_copy(
            src_ref=src,
            dst_ref=self.view(n, a, b, part),
            send_sem=self.send.at[n, kind],
            recv_sem=self.recv.at[n, kind],
            device_id={"tensor": self.at(*where)},
            device_id_type=MESH,
        )

    def go(self, *what):
        self.copy(*what).start()
        self.started.append(what)

    def landed(self, n, kind, a, b, part):
        self.copy(n, kind, a, b, part, (0, 0, 1)).wait_recv()

    def spread(self, n, k):
        r = ORDER[k]
        self.go(n, FULL_B + 2 * k, r, 0, None, (0, 1))
        self.go(n, FULL_B + 2 * k + 1, r, 0, None, (0, -1))
        self.go(n, PAIR + k, r, 0, None, (0, 0, 1))

    def own(self, n):
        return pltpu.make_async_copy(
            self.shards[n], self.outs[n].at[self.place], self.here.at[n]
        )

    def begin(self):
        for n in self.every:
            self.go(n, FULL_A, 0, 0, None, (1, 0))
            self.go(n, FULL_A + 1, 0, 0, None, (-1, 0))
            self.spread(n, 0)
        for n in self.every:
            self.own(n).start()

    def first_ring(self):
        for n in self.every:
            self.landed(n, FULL_A, -1, 0, None)
            self.go(n, HALF_A, -1, 0, 0, (1, 0))
            self.spread(n, 1)
            self.landed(n, FULL_A + 1, 1, 0, None)
            self.go(n, HALF_A + 1, 1, 0, 1, (-1, 0))
            self.spread(n, 2)

    def second_ring(self, k):
        r = ORDER[k]
        for n in self.every:
            if k == 1:
                self.landed(n, HALF_A, 2, 0, 0)
                self.landed(n, HALF_A + 1, 2, 0, 1)
                self.spread(n, 3)
            self.landed(n, FULL_B + 2 * k, r, -1, None)
            self.go(n, HALF_B + 2 * k, r, -1, 0, (0, 1))
            self.go(n, PAIR + 4 + k, r, -1, None, (0, 0, 1))
            self.landed(n, FULL_B + 2 * k + 1, r, 1, None)
            self.go(n, HALF_B + 2 * k + 1, r, 1, 1, (0, -1))
            self.go(n, PAIR + 8 + k, r, 1, None, (0, 0, 1))

    def last(self):
        for n in self.every:
            for k in range(RING):
                self.landed(n, HALF_B + 2 * k, ORDER[k], 2, 0)
                self.landed(n, HALF_B + 2 * k + 1, ORDER[k], 2, 1)
                self.go(n, PAIR + 12 + k, ORDER[k], 2, None, (0, 0, 1))

    def finish(self):
        for n in self.every:
            self.own(n).wait()
            for k in range(4 * RING):
                self.landed(n, PAIR + k, 1, 1, None)
        for what in self.started:
            self.copy(*what).wait_send()


def ring_scratch(count):
    return [
        pltpu.SemaphoreType.DMA((count, COPIES)),
        pltpu.SemaphoreType.DMA((count, COPIES)),
        pltpu.SemaphoreType.DMA((count,)),
    ]


def gather_kernel(splits, extra, *refs):
    count = len(splits)
    shards, refs = refs[:count], refs[count:]
    sent, refs = refs[:extra], refs[extra:]
    outs, refs = refs[:count], refs[count:]
    got, refs = refs[:extra], refs[extra:]
    rings = Rings(shards, outs, splits, *refs[:3])
    barrier = pltpu.get_barrier_semaphore()
    greeted = rings.greet(barrier)
    steps = []
    if extra:
        seq = lax.axis_index("seq")
        seq_size = lax.axis_size("seq")
        later = lax.rem(seq + 1, seq_size)
        for peer in (later, lax.rem(seq + seq_size - 1, seq_size)):
            pl.semaphore_signal(barrier, inc=1, device_id={"seq": peer}, device_id_type=MESH)
        greeted += 2
    pl.semaphore_wait(barrier, greeted)
    rings.begin()
    for i in range(extra):
        z = pltpu.make_async_remote_copy(
            src_ref=sent[i],
            dst_ref=got[i],
            send_sem=refs[3].at[2 * i],
            recv_sem=refs[3].at[2 * i + 1],
            device_id={"seq": later},
            device_id_type=MESH,
        )
        z.start()
        steps.append(z)
    rings.first_ring()
    for k in range(RING):
        rings.second_ring(k)
    rings.last()
    for z in steps:
        z.wait()
    rings.finish()


def gather(shards, splits, number, sent=()):
    places = lax.axis_size("tensor")
    vm = pl.BlockSpec(memory_space=pltpu.VMEM)
    anyspace = pl.BlockSpec(memory_space=pl.ANY)
    return pl.pallas_call(
        functools.partial(gather_kernel, splits, len(sent)),
        out_shape=[jax.ShapeDtypeStruct((places,) + s.shape, s.dtype) for s in shards]
        + [jax.ShapeDtypeStruct(s.shape, s.dtype) for s in sent],
        in_specs=[vm] * (len(shards) + len(sent)),
        out_specs=[anyspace] * len(shards) + [vm] * len(sent),
        scratch_shapes=ring_scratch(len(shards))
        + ([pltpu.SemaphoreType.DMA((2 * len(sent),))] if sent else []),
        compiler_params=pltpu.CompilerParams(collective_id=number, has_side_effects=True),
        name="gather_%d" % number,
    )(*shards, *sent)


def attention_kernel(
    starts_ref, q_ref, w_ref, kv_ref, out_ref, gathered_ref, kv, top, total, acc, chunk_sem, *sems
):
    place = lax.axis_index("tensor")
    rings = Rings([w_ref], [gathered_ref], [(1, w_ref.shape[1] // 2)], *sems)
    barrier = pltpu.get_barrier_semaphore()
    greeted = rings.greet(barrier)

    def fetch(i):
        w = place + i
        block = w // CHUNKS
        row = pl.multiple_of((1 - block) * TOK, TOK)
        return pltpu.make_async_copy(
            kv_ref.at[w - block * CHUNKS, pl.ds(row, TOK), :], kv.at[i], chunk_sem.at[i]
        )

    def fetch_step(i, _):
        fetch(i).start()
        return 0

    lax.fori_loop(0, CHUNKS + 1, fetch_step, 0)
    scale = math.log2(math.e) / math.sqrt(HEAD)
    group_heads = HEADS // KV_HEADS
    top[...] = jnp.full_like(top, NEG)
    total[...] = jnp.zeros_like(total)
    acc[...] = jnp.zeros_like(acc)
    pl.semaphore_wait(barrier, greeted)
    rings.begin()
    starts = starts_ref[...]
    query = lax.broadcasted_iota(jnp.int32, (STEP * TOK, TOK), 1) + CHUNKS * TOK
    local = lax.broadcasted_iota(jnp.int32, (STEP * TOK, TOK), 0)

    def step(number, _):
        first = number * STEP
        pl.when(number == 2)(rings.first_ring)
        for k in range(RING):
            pl.when(number == 3 + k)(functools.partial(rings.second_ring, k))
        pl.when(number == 8)(rings.last)
        for i in range(STEP):
            fetch(first + i).wait()
        pieces = [kv.at[first + i] for i in range(STEP)]
        pos = local + first * TOK
        allowed = (pos >= starts) & (pos <= query)
        for g in range(KV_HEADS):
            keys = jnp.concatenate([p[:, g * HEAD : (g + 1) * HEAD] for p in pieces], axis=0)
            vals = jnp.concatenate(
                [p[:, (KV_HEADS + g) * HEAD : (KV_HEADS + g + 1) * HEAD] for p in pieces], axis=0
            )
            for h in range(group_heads):
                head = g * group_heads + h
                s = lax.dot_general(
                    keys,
                    q_ref[:, head * HEAD : (head + 1) * HEAD],
                    (((1,), (1,)), ((), ())),
                    preferred_element_type=F32,
                )
                s = jnp.where(allowed, s * scale, NEG)
                old = top[head : head + 1, :]
                new = jnp.maximum(old, jnp.max(s, axis=0, keepdims=True))
                alpha = jnp.exp2(old - new)
                w = jnp.exp2(s - new)
                top[head : head + 1, :] = new
                total[head : head + 1, :] = total[head : head + 1, :] * alpha + jnp.sum(
                    w, axis=0, keepdims=True
                )
                got = lax.dot_general(
                    vals, w.astype(BF16), (((0,), (0,)), ((), ())), preferred_element_type=F32
                )
                acc[head] = acc[head] * alpha + got
        return 0

    lax.fori_loop(0, (CHUNKS + 1) // STEP, step, 0)
    for head in range(HEADS):
        out_ref[head] = (acc[head] / total[head : head + 1, :]).astype(BF16)
    rings.finish()


def attention(starts, q, w_out_t, kv_all):
    vm = pl.BlockSpec(memory_space=pltpu.VMEM)
    anyspace = pl.BlockSpec(memory_space=pl.ANY)
    return pl.pallas_call(
        attention_kernel,
        out_shape=[
            jax.ShapeDtypeStruct((HEADS, HEAD, TOK), BF16),
            jax.ShapeDtypeStruct((CHUNKS,) + w_out_t.shape, BF16),
        ],
        in_specs=[vm, vm, vm, anyspace],
        out_specs=[vm, anyspace],
        scratch_shapes=[
            pltpu.VMEM((CHUNKS + 1, TOK, kv_all.shape[2]), BF16),
            pltpu.VMEM((16, TOK), F32),
            pltpu.VMEM((16, TOK), F32),
            pltpu.VMEM((HEADS, HEAD, TOK), F32),
            pltpu.SemaphoreType.DMA((CHUNKS + 1,)),
        ]
        + ring_scratch(1),
        compiler_params=pltpu.CompilerParams(collective_id=2, has_side_effects=True),
        name="window_attention",
    )(starts, q, w_out_t, kv_all)


def body(
    tokens,
    segment_ids,
    page_table,
    attn_gain,
    w_qkv,
    w_out,
    moe_gain,
    route_ids,
    route_weight,
    w_gate,
    w_up,
    w_down,
):
    tok_rows = tokens.shape[0]
    tensor_size = lax.axis_size("tensor")
    tensor_index = lax.axis_index("tensor")
    seq_index = lax.axis_index("seq")
    query_width = HEADS * HEAD

    counts = jnp.sum(
        (segment_ids[:, None] < jnp.arange(TOK, dtype=jnp.int32)[None, :]).astype(F32), axis=0
    ).astype(BF16)
    count_rows = jnp.broadcast_to(counts[None, :], (PAGE, TOK))
    qkv_t, earlier, earlier_counts = gather(
        [w_qkv.T], [(0, w_qkv.shape[1] // 2)], 0, (tokens, count_rows)
    )
    qkv_t = qkv_t.reshape(-1, tokens.shape[1])
    normed = rms_scaled(jnp.concatenate([tokens, earlier], axis=0), attn_gain)
    nt = (((1,), (1,)), ((), ()))
    projected = lax.dot_general(normed, qkv_t, nt, preferred_element_type=F32).astype(BF16)
    kv = projected[:, query_width:]
    kvw = kv.shape[1]
    upper = jnp.arange(2 * PAGE)[:, None] < PAGE
    both_counts = jnp.where(
        upper, jnp.tile(count_rows, (2, 1)), jnp.tile(earlier_counts, (2, 1))
    )
    kv_all, counts_all = gather([kv, both_counts], [(0, tok_rows), (0, PAGE)], 1)

    own_counts = counts_all[:, 0, :].astype(F32)
    prev_counts = counts_all[:, PAGE, :].astype(F32)
    order = jnp.arange(tensor_size)[:, None]
    before = jnp.where(seq_index == 0, jnp.full_like(prev_counts, TOK), prev_counts)
    starts_of = jnp.sum(
        jnp.where(order <= tensor_index, own_counts, 0.0)
        + jnp.where(order >= tensor_index, before, 0.0),
        axis=0,
    ).astype(jnp.int32)
    starts = jnp.sum(
        jnp.where(
            segment_ids[None, :] == jnp.arange(TOK, dtype=jnp.int32)[:, None], starts_of[:, None], 0
        ),
        axis=0,
    )
    ctx, out_t = attention(
        starts[None, :], projected[:tok_rows, :query_width], w_out.T, kv_all
    )
    out_t = out_t.reshape(-1, query_width)

    pages_here = tok_rows // PAGE
    pages_block = page_table.shape[1]
    slot_ids = tensor_index * pages_here + jnp.arange(pages_here, dtype=jnp.int32)
    matches = page_table[0][None, :] == slot_ids[:, None]
    logical = jnp.sum(
        jnp.where(matches, jnp.arange(pages_block, dtype=jnp.int32)[None, :], 0), axis=1
    )
    cache_pages = jnp.stack(
        [
            lax.dynamic_slice(
                kv_all,
                (logical[i] // pages_here, (logical[i] % pages_here) * PAGE, 0),
                (1, PAGE, kvw),
            )[0]
            for i in range(pages_here)
        ]
    )

    attn_out = lax.dot_general(
        ctx.reshape(query_width, tok_rows), out_t, (((0,), (1,)), ((), ())),
        preferred_element_type=F32,
    )
    residual = (tokens.astype(F32) + attn_out).astype(BF16)
    expert_input = rms_scaled(residual, moe_gain)

    experts_all = w_gate.shape[0] * tensor_size
    capacity = max(2, 3 * tok_rows * TOP // (2 * experts_all))
    picks = route_ids.T[None] == jnp.arange(experts_all, dtype=jnp.int32)[:, None, None]
    hits = jnp.any(picks, axis=1)
    weights = jnp.sum(jnp.where(picks, route_weight.T[None], 0.0), axis=1)
    order_of = jnp.arange(tok_rows, dtype=jnp.int32)
    ahead = (order_of[:, None] < order_of[None, :]).astype(BF16)
    ranks = jnp.dot(hits.astype(BF16), ahead, preferred_element_type=F32)
    slots = jnp.arange(capacity, dtype=jnp.int32).astype(F32)[None, :, None]
    taken = jnp.logical_and(hits[:, None, :], ranks[:, None, :] == slots)
    dispatch = taken.astype(BF16).reshape(experts_all * capacity, tok_rows)
    spread = jnp.where(taken, weights[:, None, :], 0.0).reshape(experts_all * capacity, tok_rows)
    high = spread.astype(BF16)
    low = (spread - high.astype(F32)).astype(BF16)
    outgoing = jnp.dot(dispatch, expert_input, preferred_element_type=F32).astype(BF16)
    outgoing = outgoing.reshape(experts_all, capacity, expert_input.shape[1])
    arrived = lax.all_to_all(outgoing, "tensor", split_axis=0, concat_axis=0, tiled=True)
    rows_flat = arrived.reshape(-1, arrived.shape[-1])
    gate_out = jnp.dot(rows_flat, w_gate[0], preferred_element_type=F32)
    up_out = jnp.dot(rows_flat, w_up[0], preferred_element_type=F32)
    hidden = (jnp.maximum(gate_out, 0.0) * up_out).astype(BF16)
    produced = jnp.dot(hidden, w_down[0], preferred_element_type=F32).astype(BF16)
    returned = lax.all_to_all(
        produced.reshape(arrived.shape), "tensor", split_axis=0, concat_axis=0, tiled=True
    ).reshape(rows_flat.shape)
    tn = (((0,), (0,)), ((), ()))
    routed_sum = lax.dot_general(
        high, returned, tn, preferred_element_type=F32
    ) + lax.dot_general(low, returned, tn, preferred_element_type=F32)
    mixed = (residual.astype(F32) + routed_sum).astype(BF16)
    return (mixed, cache_pages)


def solution(mesh):
    return jax.shard_map(
        body,
        mesh=mesh,
        in_specs=(
            P(("seq", "tensor"), None),
            P(("seq", "tensor")),
            P("seq", None),
            P(),
            P(None, "tensor"),
            P(None, "tensor"),
            P(),
            P(("seq", "tensor"), None),
            P(("seq", "tensor"), None),
            P("tensor", None, None),
            P("tensor", None, None),
            P("tensor", None, None),
        ),
        out_specs=(P(("seq", "tensor"), None), P(("seq", "tensor"), None, None)),
        check_vma=False,
    )
```

time: 290 us -> 207 us (0.71)
  waiting for transfers between devices: 126 us -> 4.21 us
  Pallas kernels: 17 us -> 93.1 us
  between operations: 33.6 us -> 21.2 us
  local copies, waits for them, and re-layouts: 21.5 us -> 11.1 us
  other arithmetic: 14 us -> 4.91 us
  starting transfers between devices: 9.23 us -> 4.73 us
    all_gather x3 -> x0, waiting for transfers between devices: 116 us -> none  [the longest x1 43.5 us: body(): qkv_t = lax.all_gather(w_qkv.T, 'tensor', axis=0, tiled=True)]
    pallas_call x1 -> x3, Pallas kernels: 17 us -> 93.1 us  [the longest x2 67.4 us: gather(): pl.pallas_call(functools.partial(gather_kernel, splits, len(sent)), out_s...]
    ppermute x1 -> x0, waiting for transfers between devices: 8.79 us -> none  [body(): lax.ppermute(sent, 'seq', [(i, i + 1) for i in range(seq_size - 1)])]
    unnamed x32 -> x29, local copies, waits for them, and re-layouts: 12.1 us -> 6.47 us
    ppermute x1 -> x0, starting transfers between devices: 4.4 us -> none  [body(): lax.ppermute(sent, 'seq', [(i, i + 1) for i in range(seq_size - 1)])]
    all_to_all x1, waiting for transfers between devices: 0.01 us -> 4.21 us  [body(): lax.all_to_all(produced.reshape(arrived.shape), 'tensor', split_axis=0, c...]
    another operation x2 -> x0, other arithmetic: 3.25 us -> none
  transfers between devices with their start and end apart: 5 -> 1, of which waited for: 4 -> 1; matrix products, arithmetic and copies ran while one was open for 13% -> 3% of each run, Pallas kernels for 6% -> 0%
where the time goes in v3:
time: 207 us; the launch traced here: 206 us
  Pallas kernels  93.1 us (45%)
  blocking collectives  39.1 us (19%)
  matrix products  27.9 us (13%)
  between operations  21.2 us (10%)
  local copies, waits for them, and re-layouts  11.1 us (5%)
  other arithmetic  4.91 us (2%)
  starting transfers between devices  4.73 us (2%)
  waiting for transfers between devices  4.21 us (2%)
    pallas_call x2, Pallas kernels, gather(): pl.pallas_call(functools.partial(gather_kernel, splits, len(sent)), out_s...  67.4 us
    all_to_all x1, blocking collectives, body(): lax.all_to_all(outgoing, 'tensor', split_axis=0, concat_axis=0, tiled=True)  39.1 us
    pallas_call x1, Pallas kernels, attention(): pl.pallas_call(attention_kernel, out_shape=[jax.ShapeDtypeStruct((HEADS,...  25.7 us
    dot_general x1, matrix products, body(): jnp.dot(hidden, w_down[0], preferred_element_type=F32).astype(BF16)  9.12 us
    unnamed x29, local copies, waits for them, and re-layouts  6.47 us
    dot_general x1, matrix products, body(): lax.dot_general(normed, qkv_t, nt, preferred_element_type=F32).astype(BF16)  4.9 us
    all_to_all x1, starting transfers between devices, body(): lax.all_to_all(produced.reshape(arrived.shape), 'tensor', split_axis=0, c...  4.73 us
    dot_general x1, matrix products, body(): lax.dot_general(ctx.reshape(query_width, tok_rows), out_t, (((0,), (1,)),...  4.22 us
  transfers between devices with their start and end apart: 1, of which 1 were waited for; matrix products, arithmetic and copies ran while one was open for 3% of the time, Pallas kernels for 0%

profile of v3, /device:TPU:1, one launch (start us, length us, event | category | flops | bytes accessed | tf_op | source)
XLA Modules:
  0.0 206.2 jit_solution(16160686001504728585)
XLA Ops:
  0.6 0.0 copy-start
  0.7 0.9 convert_reduce_fusion
  1.6 0.6 broadcast_in_dim.109.refs_2_
  2.2 34.7 %gather_0.1 = (bf16[32,64,1536]{2,1,0:T(8,128)(2,1)}, bf16[128,1536]{1,0:T(8,128)(2,1)}, bf16[16,128]{1,0:T(8,128)(2,1)}) custom-call(bf16[64,1536]{1,0:T(8,128)(2,1)} %bitcast.72, bf16[128,1536]{1,0:T(8,128)(2,1)} %refs_1_.1, bf16[16,128]{1,0:T(8,128)(2,1)} %broadcast_in_dim.109.refs_2_), custom_call_target="tpu_custom_call" | custom-call | tf_op jit(solution)/shard_map/gather_0/pallas_call | solution.py:200
  36.9 1.4 fusion.12
  38.2 0.0 copy-start.5
  38.2 0.0 copy-start.10
  38.2 4.9 %convolution_convert_fusion.2 = bf16[256,2048]{1,0:T(8,128)(2,1)S(1)} fusion(bf16[2048,1536]{1,0:T(8,128)(2,1)} %bitcast.80, f32[1536]{0:T(1024)} %param.15, f32[256]{0:T(256)S(1)} %add_rsqrt_fusion, bf16[128,1536]{1,0:T(8,128)(2,1)} %get-tuple-element.9, bf16[128,1536]{1,0:T(8,128)(2,1)} %refs_1_.1), kind=kOutput, calls=%fused_computation.2 | convolution fusion | flops 1613889536 | bytes 8133632 | tf_op jit(solution)/shard_map/dot_general | solution.py:344
  43.2 0.7 slice.56.refs_0_
  43.9 0.8 slice.58.q_ref
  44.7 0.0 copy-done.5
  44.7 0.7 bitcast_select_fusion.refs_1_
  45.3 32.7 %gather_1.1 = (bf16[32,256,512]{2,1,0:T(8,128)(2,1)}, bf16[32,32,128]{2,1,0:T(8,128)(2,1)}) custom-call(bf16[256,512]{1,0:T(8,128)(2,1)} %slice.56.refs_0_, bf16[32,128]{1,0:T(8,128)(2,1)} %bitcast_select_fusion.refs_1_), custom_call_target="tpu_custom_call" | custom-call | tf_op jit(solution)/shard_map/gather_1/pallas_call | solution.py:200
  78.0 1.1 copy.21
  79.1 0.9 broadcast_select_fusion
  79.9 0.1 fusion.38
  80.0 0.0 copy-done.10
  80.1 0.6 select_reduce_fusion.1
  80.7 25.7 %window_attention.1 = (bf16[12,128,128]{2,1,0:T(8,128)(2,1)}, bf16[32,48,1536]{2,1,0:T(8,128)(2,1)}) custom-call(s32[1,128]{1,0:T(1,128)} %bitcast.79, bf16[128,1536]{1,0:T(8,128)(2,1)} %slice.58.q_ref, bf16[48,1536]{1,0:T(8,128)(2,1)} %bitcast.73, bf16[32,256,512]{2,1,0:T(8,128)(2,1)} %get-tuple-element.13.kv_ref), custom_call_target="tpu_custom_call" | custom-call | tf_op jit(solution)/shard_map/window_attention/pallas_call | solution.py:293
  106.4 0.0 copy-done.1
  106.4 0.0 copy-start.4
  106.4 0.0 copy-start.3
  106.4 4.2 %multiply_reduce_fusion = (f32[128]{0:T(128)S(1)}, f32[128,1536]{1,0:T(8,128)S(1)}) fusion(bf16[1536,128]{1,0:T(8,128)(2,1)} %bitcast.71, bf16[1536,1536]{1,0:T(8,128)(2,1)} %bitcast.67, bf16[128,1536]{1,0:T(8,128)(2,1)S(1)} %copy-done.1), kind=kOutput, calls=%fused_computation.24 | convolution fusion | flops 605159296 | bytes 6291968 | tf_op jit(solution)/shard_map/dot_general | solution.py:391
  110.7 0.0 copy-done.4
  110.7 0.1 fusion.36
  110.8 0.1 eq.95
  110.9 0.2 fusion.23
  111.1 0.8 convolution_convert_fusion.1
  111.9 0.0 copy-start.9
  112.0 39.1 %all_to_all.10 = bf16[32,24,1536]{2,1,0:T(8,128)(2,1)S(1)} all-to-all(bf16[32,24,1536]{2,1,0:T(8,128)(2,1)S(1)} %bitcast.66), channel_id=1, replica_groups=mesh['seq'=8,'tensor'=32] {'tensor'}, dimensions={0} | all-to-all | bytes 4718592 | tf_op jit(solution)/shard_map/all_to_all | solution.py:414
  151.1 1.4 copy-done.2
  152.4 3.4 %fusion.6 = f32[768,768]{1,0:T(8,128)} fusion(bf16[768,1536]{1,0:T(8,128)(2,1)S(1)} %bitcast.69, bf16[1,1536,768]{2,1,0:T(8,128)(2,1)S(1)} %copy-done.9), kind=kOutput, calls=%fused_computation.12 | convolution fusion | flops 1811939328 | bytes 7077888 | tf_op jit(solution)/shard_map/dot_general | solution.py:417
  155.9 0.0 copy-done
  155.9 9.1 %convolution_convert_fusion = bf16[768,1536]{1,0:T(8,128)(2,1)} fusion(bf16[1,768,1536]{2,1,0:T(8,128)(2,1)S(1)} %copy-done, f32[768,768]{1,0:T(8,128)} %fusion.6, bf16[768,1536]{1,0:T(8,128)(2,1)} %bitcast.70, bf16[1,1536,768]{2,1,0:T(8,128)(2,1)} %param.21), kind=kOutput, calls=%fused_computation | convolution fusion | flops 3626827776 | bytes 11796480 | tf_op jit(solution)/shard_map/dot_general | solution.py:419
  165.0 4.7 %all-to-all-start.1 = ((bf16[32,24,1536]{2,1,0:T(8,128)(2,1)}), bf16[32,24,1536]{2,1,0:T(8,128)(2,1)}, u32[]{:S(2)}, u32[]{:S(2)}) async-start(bf16[32,24,1536]{2,1,0:T(8,128)(2,1)} %bitcast.68), calls=%async_computation.1 | async-start | bytes 4718592 | tf_op jit(solution)/shard_map/all_to_all | solution.py:420
  169.8 0.2 select_reduce_fusion.2
  169.9 0.7 fusion.43
  191.0 0.7 constant_dynamic-update-slice_fusion.7
  191.7 0.7 constant_dynamic-update-slice_fusion.6
  192.4 0.7 constant_dynamic-update-slice_fusion.5
  193.1 0.7 constant_dynamic-update-slice_fusion.4
  193.9 0.7 constant_dynamic-update-slice_fusion.3
  194.6 0.7 constant_dynamic-update-slice_fusion.2
  195.3 0.7 constant_dynamic-update-slice_fusion.1
  196.0 0.7 constant_dynamic-update-slice_fusion
  196.8 4.2 %all-to-all-done.1 = bf16[32,24,1536]{2,1,0:T(8,128)(2,1)} async-done(((bf16[32,24,1536]{2,1,0:T(8,128)(2,1)}), bf16[32,24,1536]{2,1,0:T(8,128)(2,1)}, u32[]{:S(2)}, u32[]{:S(2)}) %all-to-all-start.1) | async-done | bytes 2359328 | tf_op jit(solution)/shard_map/all_to_all | solution.py:420
  201.0 2.2 %convolution_bitcast_fusion = f32[128,1536]{1,0:T(8,128)S(1)} fusion(bf16[32,24,1536]{2,1,0:T(8,128)(2,1)} %all-to-all-done.1, f32[32,128]{1,0:T(8,128)S(1)} %select_reduce_fusion, f32[32,128]{1,0:T(8,128)S(1)} %fusion.36, f32[24]{0:T(128)S(1)} %iota_convert_fusion, pred[32,128]{1,0:T(8,128)(4,1)S(1)} %fusion.35), kind=kOutput, calls=%fused_computation.4 | convolution fusion | flops 302678016 | bytes 3182688 | tf_op jit(solution)/shard_map/dot_general | solution.py:426
  203.2 3.0 %fusion.2 = bf16[128,1536]{1,0:T(8,128)(2,1)} fusion(f32[128,1536]{1,0:T(8,128)S(1)} %get-tuple-element.25, f32[128,1536]{1,0:T(8,128)S(1)} %convolution_bitcast_fusion, bf16[32,24,1536]{2,1,0:T(8,128)(2,1)} %all-to-all-done.1, f32[32,128]{1,0:T(8,128)S(1)} %select_reduce_fusion, f32[32,128]{1,0:T(8,128)S(1)} %fusion.36, f32[24]{0:T(128)S(1)} %iota_convert_fusion, ...), kind=kOutput, calls=%fused_computation.8 | convolution fusion | flops 302874624 | bytes 4362336 | tf_op jit(solution)/shard_map/dot_general | solution.py:424
  (20 shorter events, 0.1 us)
Async XLA Ops:
  0.6 155.2 %copy-start = (bf16[1,768,1536]{2,1,0:T(8,128)(2,1)S(1)}, bf16[1,768,1536]{2,1,0:T(8,128)(2,1)}, u32[]{:S(2)}) copy-start(bf16[1,768,1536]{2,1,0:T(8,128)(2,1)} %param.23) | copy-start | bytes 7077892
  38.2 6.4 %copy-start.5 = (bf16[16,128]{1,0:T(8,128)(2,1)S(1)}, bf16[16,128]{1,0:T(8,128)(2,1)}, u32[]{:S(2)}) copy-start(bf16[16,128]{1,0:T(8,128)(2,1)} %get-tuple-element.11) | copy-start | bytes 12292
  38.2 41.8 %copy-start.10 = (s32[128]{0:T(128)S(1)}, s32[128]{0:T(128)}, u32[]{:S(2)}) copy-start(s32[128]{0:T(128)} %param.13) | copy-start | bytes 1540
  80.7 25.7 %copy-start.1 = (bf16[128,1536]{1,0:T(8,128)(2,1)S(1)}, bf16[128,1536]{1,0:T(8,128)(2,1)}, u32[]{:S(2)}) copy-start(bf16[128,1536]{1,0:T(8,128)(2,1)} %refs_1_.1) | copy-start | bytes 1179652
  106.4 4.3 %copy-start.4 = (s32[128,4]{0,1:T(4,128)S(1)}, s32[128,4]{0,1:T(4,128)}, u32[]{:S(2)}) copy-start(s32[128,4]{0,1:T(4,128)} %param.19) | copy-start | bytes 6148
  106.4 4.7 %copy-start.3 = (f32[1536]{0:T(1024)S(1)}, f32[1536]{0:T(1024)}, u32[]{:S(2)}) copy-start(f32[1536]{0:T(1024)} %param.18) | copy-start | bytes 18436
  111.9 40.5 %copy-start.9 = (bf16[1,1536,768]{2,1,0:T(8,128)(2,1)S(1)}, bf16[1,1536,768]{2,1,0:T(8,128)(2,1)}, u32[]{:S(2)}) copy-start(bf16[1,1536,768]{2,1,0:T(8,128)(2,1)} %param.22) | copy-start | bytes 7077892
  151.1 1.4 copy-start.2
  165.0 4.8 %copy-start.8 = (s32[1,256]{1,0:T(1,128)S(1)}, s32[1,256]{1,0:T(1,128)}, u32[]{:S(2)}) copy-start(s32[1,256]{1,0:T(1,128)} %param.14) | copy-start | bytes 3076
  165.0 31.7 %copy-start.6 = (f32[128,4]{0,1:T(4,128)S(1)}, f32[128,4]{0,1:T(4,128)}, u32[]{:S(2)}) copy-start(f32[128,4]{0,1:T(4,128)} %param.20) | copy-start | bytes 6148
  165.0 36.0 %all-to-all-start.1 = ((bf16[32,24,1536]{2,1,0:T(8,128)(2,1)}), bf16[32,24,1536]{2,1,0:T(8,128)(2,1)}, u32[]{:S(2)}, u32[]{:S(2)}) async-start(bf16[32,24,1536]{2,1,0:T(8,128)(2,1)} %bitcast.68), calls=%async_computation.1 | async-start | bytes 4718592 | tf_op jit(solution)/shard_map/all_to_all | solution.py:420
  196.7 9.5 %copy-start.7 = (bf16[8,16,512]{2,1,0:T(8,128)(2,1)}, bf16[8,16,512]{2,1,0:T(8,128)(2,1)S(1)}, u32[]{:S(2)}) copy-start(bf16[8,16,512]{2,1,0:T(8,128)(2,1)S(1)} %constant_dynamic-update-slice_fusion) | copy-start | bytes 393220

commit v4 on v3

--- a/solution.py
+++ b/solution.py
@@ -38,7 +38,8 @@
 
 
 class Rings:
-    def __init__(self, shards, outs, splits, send, recv, here):
+    def __init__(self, shards, outs, splits, send, recv, here, rows=(), columns=False):
+        self.rows, self.columns = rows, columns
         self.shards, self.outs, self.splits = shards, outs, splits
         self.send, self.recv, self.here = send, recv, here
         self.place = lax.axis_index("tensor")
@@ -54,6 +55,9 @@
         y = lax.rem(self.py + a * core + b * (1 - core) + RING, RING)
         return (y * RING + x) * 2 + ((1 - core) if flip else core)
 
+    def row(self, a):
+        return lax.rem(self.px * (1 - self.core) + self.py * self.core + a + RING, RING)
+
     def greet(self, barrier):
         for where in ((1, 0), (-1, 0), (0, 1), (0, -1), (0, 0, 1)):
             pl.semaphore_signal(
@@ -62,7 +66,7 @@
         return 5
 
     def view(self, n, a, b, part):
-        ref = self.outs[n].at[self.at(a, b)]
+        ref = self.outs[n].at[self.row(a) if n in self.rows else self.at(a, b)]
         if part is None:
             return ref
         axis, cut = self.splits[n]
@@ -71,7 +75,10 @@
         return ref.at[span, :] if axis == 0 else ref.at[:, span]
 
     def copy(self, n, kind, a, b, part, where):
-        src = self.shards[n] if (a == 0 and b == 0) else self.view(n, a, b, part)
+        if self.columns and b == 0:
+            src = self.shards[n].at[self.row(a)]
+        else:
+            src = self.shards[n] if (a == 0 and b == 0) else self.view(n, a, b, part)
         return pltpu.make_async_remote_copy(
             src_ref=src,
             dst_ref=self.view(n, a, b, part),
@@ -89,23 +96,36 @@
         self.copy(n, kind, a, b, part, (0, 0, 1)).wait_recv()
 
     def spread(self, n, k):
+        if n in self.rows:
+            return
         r = ORDER[k]
         self.go(n, FULL_B + 2 * k, r, 0, None, (0, 1))
         self.go(n, FULL_B + 2 * k + 1, r, 0, None, (0, -1))
         self.go(n, PAIR + k, r, 0, None, (0, 0, 1))
 
     def own(self, n):
-        return pltpu.make_async_copy(
-            self.shards[n], self.outs[n].at[self.place], self.here.at[n]
-        )
+        if self.columns:
+            return [
+                pltpu.make_async_copy(
+                    self.shards[n].at[self.row(r)], self.outs[n].at[self.at(r, 0)], self.here.at[k]
+                )
+                for k, r in enumerate(ORDER)
+            ]
+        slot = self.row(0) if n in self.rows else self.place
+        return [pltpu.make_async_copy(self.shards[n], self.outs[n].at[slot], self.here.at[n])]
 
     def begin(self):
         for n in self.every:
-            self.go(n, FULL_A, 0, 0, None, (1, 0))
-            self.go(n, FULL_A + 1, 0, 0, None, (-1, 0))
-            self.spread(n, 0)
-        for n in self.every:
-            self.own(n).start()
+            if self.columns:
+                for k in range(RING):
+                    self.spread(n, k)
+            else:
+                self.go(n, FULL_A, 0, 0, None, (1, 0))
+                self.go(n, FULL_A + 1, 0, 0, None, (-1, 0))
+                self.spread(n, 0)
+        for n in self.every:
+            for c in self.own(n):
+                c.start()
 
     def first_ring(self):
         for n in self.every:
@@ -119,10 +139,12 @@
     def second_ring(self, k):
         r = ORDER[k]
         for n in self.every:
-            if k == 1:
+            if k == 1 and not self.columns:
                 self.landed(n, HALF_A, 2, 0, 0)
                 self.landed(n, HALF_A + 1, 2, 0, 1)
                 self.spread(n, 3)
+            if n in self.rows:
+                continue
             self.landed(n, FULL_B + 2 * k, r, -1, None)
             self.go(n, HALF_B + 2 * k, r, -1, 0, (0, 1))
             self.go(n, PAIR + 4 + k, r, -1, None, (0, 0, 1))
@@ -132,15 +154,16 @@
 
     def last(self):
         for n in self.every:
-            for k in range(RING):
+            for k in range(0 if n in self.rows else RING):
                 self.landed(n, HALF_B + 2 * k, ORDER[k], 2, 0)
                 self.landed(n, HALF_B + 2 * k + 1, ORDER[k], 2, 1)
                 self.go(n, PAIR + 12 + k, ORDER[k], 2, None, (0, 0, 1))
 
     def finish(self):
         for n in self.every:
-            self.own(n).wait()
-            for k in range(4 * RING):
+            for c in self.own(n):
+                c.wait()
+            for k in range(0 if n in self.rows else 4 * RING):
                 self.landed(n, PAIR + k, 1, 1, None)
         for what in self.started:
             self.copy(*what).wait_send()
@@ -150,17 +173,17 @@
     return [
         pltpu.SemaphoreType.DMA((count, COPIES)),
         pltpu.SemaphoreType.DMA((count, COPIES)),
-        pltpu.SemaphoreType.DMA((count,)),
+        pltpu.SemaphoreType.DMA((max(count, RING),)),
     ]
 
 
-def gather_kernel(splits, extra, *refs):
+def gather_kernel(splits, extra, rows, *refs):
     count = len(splits)
     shards, refs = refs[:count], refs[count:]
     sent, refs = refs[:extra], refs[extra:]
     outs, refs = refs[:count], refs[count:]
     got, refs = refs[:extra], refs[extra:]
-    rings = Rings(shards, outs, splits, *refs[:3])
+    rings = Rings(shards, outs, splits, *refs[:3], rows=rows)
     barrier = pltpu.get_barrier_semaphore()
     greeted = rings.greet(barrier)
     steps = []
@@ -193,13 +216,16 @@
     rings.finish()
 
 
-def gather(shards, splits, number, sent=()):
+def gather(shards, splits, number, sent=(), rows=()):
     places = lax.axis_size("tensor")
     vm = pl.BlockSpec(memory_space=pltpu.VMEM)
     anyspace = pl.BlockSpec(memory_space=pl.ANY)
     return pl.pallas_call(
-        functools.partial(gather_kernel, splits, len(sent)),
-        out_shape=[jax.ShapeDtypeStruct((places,) + s.shape, s.dtype) for s in shards]
+        functools.partial(gather_kernel, splits, len(sent), rows),
+        out_shape=[
+            jax.ShapeDtypeStruct((RING if n in rows else places,) + s.shape, s.dtype)
+            for n, s in enumerate(shards)
+        ]
         + [jax.ShapeDtypeStruct(s.shape, s.dtype) for s in sent],
         in_specs=[vm] * (len(shards) + len(sent)),
         out_specs=[anyspace] * len(shards) + [vm] * len(sent),
@@ -214,7 +240,7 @@
     starts_ref, q_ref, w_ref, kv_ref, out_ref, gathered_ref, kv, top, total, acc, chunk_sem, *sems
 ):
     place = lax.axis_index("tensor")
-    rings = Rings([w_ref], [gathered_ref], [(1, w_ref.shape[1] // 2)], *sems)
+    rings = Rings([w_ref], [gathered_ref], [(1, w_ref.shape[2] // 2)], *sems, columns=True)
     barrier = pltpu.get_barrier_semaphore()
     greeted = rings.greet(barrier)
 
@@ -244,10 +270,9 @@
 
     def step(number, _):
         first = number * STEP
-        pl.when(number == 2)(rings.first_ring)
         for k in range(RING):
-            pl.when(number == 3 + k)(functools.partial(rings.second_ring, k))
-        pl.when(number == 8)(rings.last)
+            pl.when(number == 2 + k)(functools.partial(rings.second_ring, k))
+        pl.when(number == 9)(rings.last)
         for i in range(STEP):
             fetch(first + i).wait()
         pieces = [kv.at[first + i] for i in range(STEP)]
@@ -287,14 +312,14 @@
     rings.finish()
 
 
-def attention(starts, q, w_out_t, kv_all):
+def attention(starts, q, w_rows, kv_all):
     vm = pl.BlockSpec(memory_space=pltpu.VMEM)
     anyspace = pl.BlockSpec(memory_space=pl.ANY)
     return pl.pallas_call(
         attention_kernel,
         out_shape=[
             jax.ShapeDtypeStruct((HEADS, HEAD, TOK), BF16),
-            jax.ShapeDtypeStruct((CHUNKS,) + w_out_t.shape, BF16),
+            jax.ShapeDtypeStruct((CHUNKS,) + w_rows.shape[1:], BF16),
         ],
         in_specs=[vm, vm, vm, anyspace],
         out_specs=[vm, anyspace],
@@ -308,7 +333,7 @@
         + ring_scratch(1),
         compiler_params=pltpu.CompilerParams(collective_id=2, has_side_effects=True),
         name="window_attention",
-    )(starts, q, w_out_t, kv_all)
+    )(starts, q, w_rows, kv_all)
 
 
 def body(
@@ -348,7 +373,12 @@
     both_counts = jnp.where(
         upper, jnp.tile(count_rows, (2, 1)), jnp.tile(earlier_counts, (2, 1))
     )
-    kv_all, counts_all = gather([kv, both_counts], [(0, tok_rows), (0, PAGE)], 1)
+    kv_all, counts_all, w_rows = gather(
+        [kv, both_counts, w_out.T],
+        [(0, tok_rows), (0, PAGE), (1, query_width // 2)],
+        1,
+        rows=(2,),
+    )
 
     own_counts = counts_all[:, 0, :].astype(F32)
     prev_counts = counts_all[:, PAGE, :].astype(F32)
@@ -366,7 +396,7 @@
         axis=0,
     )
     ctx, out_t = attention(
-        starts[None, :], projected[:tok_rows, :query_width], w_out.T, kv_all
+        starts[None, :], projected[:tok_rows, :query_width], w_rows, kv_all
     )
     out_t = out_t.reshape(-1, query_width)
 

time: 207 us -> 202 us (0.976)
  Pallas kernels: 93.1 us -> 90.5 us
  blocking collectives: 39.1 us -> 36.7 us
    pallas_call x1, Pallas kernels: 25.7 us -> 21.7 us  [attention(): pl.pallas_call(attention_kernel, out_shape=[jax.ShapeDtypeStruct((HEADS,...]
    all_to_all x1, blocking collectives: 39.1 us -> 36.7 us  [body(): lax.all_to_all(outgoing, 'tensor', split_axis=0, concat_axis=0, tiled=True)]
where the time goes in v4:
time: 202 us; the launch traced here: 201 us
  Pallas kernels  90.5 us (45%)
  blocking collectives  36.7 us (18%)
  matrix products  27.9 us (14%)
  between operations  21.2 us (10%)
  local copies, waits for them, and re-layouts  11.1 us (5%)
  other arithmetic  4.91 us (2%)
  starting transfers between devices  4.73 us (2%)
  waiting for transfers between devices  4.22 us (2%)
    pallas_call x2, Pallas kernels, gather(): pl.pallas_call(functools.partial(gather_kernel, splits, len(sent), rows),...  68.8 us
    all_to_all x1, blocking collectives, body(): lax.all_to_all(outgoing, 'tensor', split_axis=0, concat_axis=0, tiled=True)  36.7 us
    pallas_call x1, Pallas kernels, attention(): pl.pallas_call(attention_kernel, out_shape=[jax.ShapeDtypeStruct((HEADS,...  21.7 us
    dot_general x1, matrix products, body(): jnp.dot(hidden, w_down[0], preferred_element_type=F32).astype(BF16)  9.12 us
    unnamed x29, local copies, waits for them, and re-layouts  6.47 us
    dot_general x1, matrix products, body(): lax.dot_general(normed, qkv_t, nt, preferred_element_type=F32).astype(BF16)  4.91 us
    all_to_all x1, starting transfers between devices, body(): lax.all_to_all(produced.reshape(arrived.shape), 'tensor', split_axis=0, c...  4.73 us
    all_to_all x1, waiting for transfers between devices, body(): lax.all_to_all(produced.reshape(arrived.shape), 'tensor', split_axis=0, c...  4.22 us
  transfers between devices with their start and end apart: 1, of which 1 were waited for; matrix products, arithmetic and copies ran while one was open for 3% of the time, Pallas kernels for 0%

profile of v4, /device:TPU:1, one launch (start us, length us, event | category | flops | bytes accessed | tf_op | source)
XLA Modules:
  0.0 201.3 jit_solution(13717079415912574990)
XLA Ops:
  0.6 0.0 copy-start
  0.7 0.9 convert_reduce_fusion
  1.6 0.6 broadcast_in_dim.109.refs_2_
  2.2 34.7 %gather_0.1 = (bf16[32,64,1536]{2,1,0:T(8,128)(2,1)}, bf16[128,1536]{1,0:T(8,128)(2,1)}, bf16[16,128]{1,0:T(8,128)(2,1)}) custom-call(bf16[64,1536]{1,0:T(8,128)(2,1)} %bitcast.72, bf16[128,1536]{1,0:T(8,128)(2,1)} %refs_1_.1, bf16[16,128]{1,0:T(8,128)(2,1)} %broadcast_in_dim.109.refs_2_), custom_call_target="tpu_custom_call" | custom-call | tf_op jit(solution)/shard_map/gather_0/pallas_call | solution.py:223
  36.9 1.4 fusion.12
  38.3 0.0 copy-start.5
  38.3 0.0 copy-start.10
  38.3 4.9 %convolution_convert_fusion.2 = bf16[256,2048]{1,0:T(8,128)(2,1)S(1)} fusion(bf16[2048,1536]{1,0:T(8,128)(2,1)} %bitcast.80, f32[1536]{0:T(1024)} %param.15, f32[256]{0:T(256)S(1)} %add_rsqrt_fusion, bf16[128,1536]{1,0:T(8,128)(2,1)} %get-tuple-element.10, bf16[128,1536]{1,0:T(8,128)(2,1)} %refs_1_.1), kind=kOutput, calls=%fused_computation.2 | convolution fusion | flops 1613889536 | bytes 8133632 | tf_op jit(solution)/shard_map/dot_general | solution.py:369
  43.2 0.7 slice.56.refs_0_
  43.9 0.8 slice.58.q_ref
  44.7 0.0 copy-done.5
  44.7 0.7 bitcast_select_fusion.refs_1_
  45.4 34.1 %gather_1.1 = (bf16[32,256,512]{2,1,0:T(8,128)(2,1)}, bf16[32,32,128]{2,1,0:T(8,128)(2,1)}, bf16[4,48,1536]{2,1,0:T(8,128)(2,1)}) custom-call(bf16[256,512]{1,0:T(8,128)(2,1)} %slice.56.refs_0_, bf16[32,128]{1,0:T(8,128)(2,1)} %bitcast_select_fusion.refs_1_, bf16[48,1536]{1,0:T(8,128)(2,1)} %bitcast.73), custom_call_target="tpu_custom_call" | custom-call | tf_op jit(solution)/shard_map/gather_1/pallas_call | solution.py:223
  79.5 1.1 copy.21
  80.6 0.9 broadcast_select_fusion
  81.4 0.1 fusion.38
  81.5 0.0 copy-done.10
  81.6 0.6 select_reduce_fusion.1
  82.2 21.7 %window_attention.1 = (bf16[12,128,128]{2,1,0:T(8,128)(2,1)}, bf16[32,48,1536]{2,1,0:T(8,128)(2,1)}) custom-call(s32[1,128]{1,0:T(1,128)} %bitcast.79, bf16[128,1536]{1,0:T(8,128)(2,1)} %slice.58.q_ref, bf16[4,48,1536]{2,1,0:T(8,128)(2,1)} %get-tuple-element.14.w_ref, bf16[32,256,512]{2,1,0:T(8,128)(2,1)} %get-tuple-element.15.kv_ref), custom_call_target="tpu_custom_call" | custom-call | tf_op jit(solution)/shard_map/window_attention/pallas_call | solution.py:318
  103.9 0.0 copy-done.1
  103.9 0.0 copy-start.4
  103.9 0.0 copy-start.3
  103.9 4.2 %multiply_reduce_fusion = (f32[128]{0:T(128)S(1)}, f32[128,1536]{1,0:T(8,128)S(1)}) fusion(bf16[1536,128]{1,0:T(8,128)(2,1)} %bitcast.71, bf16[1536,1536]{1,0:T(8,128)(2,1)} %bitcast.67, bf16[128,1536]{1,0:T(8,128)(2,1)S(1)} %copy-done.1), kind=kOutput, calls=%fused_computation.24 | convolution fusion | flops 605159296 | bytes 6291968 | tf_op jit(solution)/shard_map/dot_general | solution.py:421
  108.1 0.0 copy-done.4
  108.1 0.1 fusion.36
  108.3 0.1 eq.95
  108.4 0.2 fusion.23
  108.6 0.8 convolution_convert_fusion.1
  109.4 0.0 copy-start.9
  109.4 36.7 %all_to_all.10 = bf16[32,24,1536]{2,1,0:T(8,128)(2,1)S(1)} all-to-all(bf16[32,24,1536]{2,1,0:T(8,128)(2,1)S(1)} %bitcast.66), channel_id=1, replica_groups=mesh['seq'=8,'tensor'=32] {'tensor'}, dimensions={0} | all-to-all | bytes 4718592 | tf_op jit(solution)/shard_map/all_to_all | solution.py:444
  146.1 1.4 copy-done.2
  147.5 3.4 %fusion.6 = f32[768,768]{1,0:T(8,128)} fusion(bf16[768,1536]{1,0:T(8,128)(2,1)S(1)} %bitcast.69, bf16[1,1536,768]{2,1,0:T(8,128)(2,1)S(1)} %copy-done.9), kind=kOutput, calls=%fused_computation.12 | convolution fusion | flops 1811939328 | bytes 7077888 | tf_op jit(solution)/shard_map/dot_general | solution.py:447
  150.9 0.0 copy-done
  150.9 9.1 %convolution_convert_fusion = bf16[768,1536]{1,0:T(8,128)(2,1)} fusion(bf16[1,768,1536]{2,1,0:T(8,128)(2,1)S(1)} %copy-done, f32[768,768]{1,0:T(8,128)} %fusion.6, bf16[768,1536]{1,0:T(8,128)(2,1)} %bitcast.70, bf16[1,1536,768]{2,1,0:T(8,128)(2,1)} %param.21), kind=kOutput, calls=%fused_computation | convolution fusion | flops 3626827776 | bytes 11796480 | tf_op jit(solution)/shard_map/dot_general | solution.py:449
  160.0 4.7 %all-to-all-start.1 = ((bf16[32,24,1536]{2,1,0:T(8,128)(2,1)}), bf16[32,24,1536]{2,1,0:T(8,128)(2,1)}, u32[]{:S(2)}, u32[]{:S(2)}) async-start(bf16[32,24,1536]{2,1,0:T(8,128)(2,1)} %bitcast.68), calls=%async_computation.1 | async-start | bytes 4718592 | tf_op jit(solution)/shard_map/all_to_all | solution.py:450
  164.8 0.2 select_reduce_fusion.2
  165.0 0.7 fusion.43
  186.0 0.7 constant_dynamic-update-slice_fusion.7
  186.7 0.7 constant_dynamic-update-slice_fusion.6
  187.5 0.7 constant_dynamic-update-slice_fusion.5
  188.2 0.7 constant_dynamic-update-slice_fusion.4
  188.9 0.7 constant_dynamic-update-slice_fusion.3
  189.6 0.7 constant_dynamic-update-slice_fusion.2
  190.3 0.7 constant_dynamic-update-slice_fusion.1
  191.1 0.7 constant_dynamic-update-slice_fusion
  191.8 4.2 %all-to-all-done.1 = bf16[32,24,1536]{2,1,0:T(8,128)(2,1)} async-done(((bf16[32,24,1536]{2,1,0:T(8,128)(2,1)}), bf16[32,24,1536]{2,1,0:T(8,128)(2,1)}, u32[]{:S(2)}, u32[]{:S(2)}) %all-to-all-start.1) | async-done | bytes 2359328 | tf_op jit(solution)/shard_map/all_to_all | solution.py:450
  196.0 2.2 %convolution_bitcast_fusion = f32[128,1536]{1,0:T(8,128)S(1)} fusion(bf16[32,24,1536]{2,1,0:T(8,128)(2,1)} %all-to-all-done.1, f32[32,128]{1,0:T(8,128)S(1)} %select_reduce_fusion, f32[32,128]{1,0:T(8,128)S(1)} %fusion.36, f32[24]{0:T(128)S(1)} %iota_convert_fusion, pred[32,128]{1,0:T(8,128)(4,1)S(1)} %fusion.35), kind=kOutput, calls=%fused_computation.4 | convolution fusion | flops 302678016 | bytes 3182688 | tf_op jit(solution)/shard_map/dot_general | solution.py:456
  198.3 3.0 %fusion.2 = bf16[128,1536]{1,0:T(8,128)(2,1)} fusion(f32[128,1536]{1,0:T(8,128)S(1)} %get-tuple-element.27, f32[128,1536]{1,0:T(8,128)S(1)} %convolution_bitcast_fusion, bf16[32,24,1536]{2,1,0:T(8,128)(2,1)} %all-to-all-done.1, f32[32,128]{1,0:T(8,128)S(1)} %select_reduce_fusion, f32[32,128]{1,0:T(8,128)S(1)} %fusion.36, f32[24]{0:T(128)S(1)} %iota_convert_fusion, ...), kind=kOutput, calls=%fused_computation.8 | convolution fusion | flops 302874624 | bytes 4362336 | tf_op jit(solution)/shard_map/dot_general | solution.py:454
  (20 shorter events, 0.1 us)
Async XLA Ops:
  0.6 150.3 %copy-start = (bf16[1,768,1536]{2,1,0:T(8,128)(2,1)S(1)}, bf16[1,768,1536]{2,1,0:T(8,128)(2,1)}, u32[]{:S(2)}) copy-start(bf16[1,768,1536]{2,1,0:T(8,128)(2,1)} %param.23) | copy-start | bytes 7077892
  38.3 6.4 %copy-start.5 = (bf16[16,128]{1,0:T(8,128)(2,1)S(1)}, bf16[16,128]{1,0:T(8,128)(2,1)}, u32[]{:S(2)}) copy-start(bf16[16,128]{1,0:T(8,128)(2,1)} %get-tuple-element.12) | copy-start | bytes 12292
  38.3 43.3 %copy-start.10 = (s32[128]{0:T(128)S(1)}, s32[128]{0:T(128)}, u32[]{:S(2)}) copy-start(s32[128]{0:T(128)} %param.13) | copy-start | bytes 1540
  82.2 21.7 %copy-start.1 = (bf16[128,1536]{1,0:T(8,128)(2,1)S(1)}, bf16[128,1536]{1,0:T(8,128)(2,1)}, u32[]{:S(2)}) copy-start(bf16[128,1536]{1,0:T(8,128)(2,1)} %refs_1_.1) | copy-start | bytes 1179652
  103.9 4.2 %copy-start.4 = (s32[128,4]{0,1:T(4,128)S(1)}, s32[128,4]{0,1:T(4,128)}, u32[]{:S(2)}) copy-start(s32[128,4]{0,1:T(4,128)} %param.19) | copy-start | bytes 6148
  103.9 4.7 %copy-start.3 = (f32[1536]{0:T(1024)S(1)}, f32[1536]{0:T(1024)}, u32[]{:S(2)}) copy-start(f32[1536]{0:T(1024)} %param.18) | copy-start | bytes 18436
  109.4 38.1 %copy-start.9 = (bf16[1,1536,768]{2,1,0:T(8,128)(2,1)S(1)}, bf16[1,1536,768]{2,1,0:T(8,128)(2,1)}, u32[]{:S(2)}) copy-start(bf16[1,1536,768]{2,1,0:T(8,128)(2,1)} %param.22) | copy-start | bytes 7077892
  146.1 1.4 copy-start.2
  160.0 4.8 %copy-start.8 = (s32[1,256]{1,0:T(1,128)S(1)}, s32[1,256]{1,0:T(1,128)}, u32[]{:S(2)}) copy-start(s32[1,256]{1,0:T(1,128)} %param.14) | copy-start | bytes 3076
  160.0 31.7 %copy-start.6 = (f32[128,4]{0,1:T(4,128)S(1)}, f32[128,4]{0,1:T(4,128)}, u32[]{:S(2)}) copy-start(f32[128,4]{0,1:T(4,128)} %param.20) | copy-start | bytes 6148
  160.0 36.0 %all-to-all-start.1 = ((bf16[32,24,1536]{2,1,0:T(8,128)(2,1)}), bf16[32,24,1536]{2,1,0:T(8,128)(2,1)}, u32[]{:S(2)}, u32[]{:S(2)}) async-start(bf16[32,24,1536]{2,1,0:T(8,128)(2,1)} %bitcast.68), calls=%async_computation.1 | async-start | bytes 4718592 | tf_op jit(solution)/shard_map/all_to_all | solution.py:450
  191.8 9.5 %copy-start.7 = (bf16[8,16,512]{2,1,0:T(8,128)(2,1)}, bf16[8,16,512]{2,1,0:T(8,128)(2,1)S(1)}, u32[]{:S(2)}) copy-start(bf16[8,16,512]{2,1,0:T(8,128)(2,1)S(1)} %constant_dynamic-update-slice_fusion) | copy-start | bytes 393220

commit v5 on v4

--- a/solution.py
+++ b/solution.py
@@ -183,6 +183,10 @@
     sent, refs = refs[:extra], refs[extra:]
     outs, refs = refs[:count], refs[count:]
     got, refs = refs[:extra], refs[extra:]
+    shards = [
+        s.at[:, pl.ds(s.shape[1] - o.shape[-1], o.shape[-1])] if s.shape[1] > o.shape[-1] else s
+        for s, o in zip(shards, outs)
+    ]
     rings = Rings(shards, outs, splits, *refs[:3], rows=rows)
     barrier = pltpu.get_barrier_semaphore()
     greeted = rings.greet(barrier)
@@ -216,14 +220,17 @@
     rings.finish()
 
 
-def gather(shards, splits, number, sent=(), rows=()):
+def gather(shards, splits, number, sent=(), rows=(), widths=None):
     places = lax.axis_size("tensor")
     vm = pl.BlockSpec(memory_space=pltpu.VMEM)
     anyspace = pl.BlockSpec(memory_space=pl.ANY)
     return pl.pallas_call(
         functools.partial(gather_kernel, splits, len(sent), rows),
         out_shape=[
-            jax.ShapeDtypeStruct((RING if n in rows else places,) + s.shape, s.dtype)
+            jax.ShapeDtypeStruct(
+                (RING if n in rows else places, s.shape[0], widths[n] if widths else s.shape[1]),
+                s.dtype,
+            )
             for n, s in enumerate(shards)
         ]
         + [jax.ShapeDtypeStruct(s.shape, s.dtype) for s in sent],
@@ -287,7 +294,7 @@
                 head = g * group_heads + h
                 s = lax.dot_general(
                     keys,
-                    q_ref[:, head * HEAD : (head + 1) * HEAD],
+                    q_ref[:TOK, head * HEAD : (head + 1) * HEAD],
                     (((1,), (1,)), ((), ())),
                     preferred_element_type=F32,
                 )
@@ -367,27 +374,27 @@
     normed = rms_scaled(jnp.concatenate([tokens, earlier], axis=0), attn_gain)
     nt = (((1,), (1,)), ((), ()))
     projected = lax.dot_general(normed, qkv_t, nt, preferred_element_type=F32).astype(BF16)
-    kv = projected[:, query_width:]
-    kvw = kv.shape[1]
+    kvw = projected.shape[1] - query_width
     upper = jnp.arange(2 * PAGE)[:, None] < PAGE
     both_counts = jnp.where(
         upper, jnp.tile(count_rows, (2, 1)), jnp.tile(earlier_counts, (2, 1))
     )
     kv_all, counts_all, w_rows = gather(
-        [kv, both_counts, w_out.T],
+        [projected, both_counts, w_out.T],
         [(0, tok_rows), (0, PAGE), (1, query_width // 2)],
         1,
         rows=(2,),
-    )
-
-    own_counts = counts_all[:, 0, :].astype(F32)
-    prev_counts = counts_all[:, PAGE, :].astype(F32)
-    order = jnp.arange(tensor_size)[:, None]
-    before = jnp.where(seq_index == 0, jnp.full_like(prev_counts, TOK), prev_counts)
-    starts_of = jnp.sum(
-        jnp.where(order <= tensor_index, own_counts, 0.0)
-        + jnp.where(order >= tensor_index, before, 0.0),
-        axis=0,
+        widths=(kvw, TOK, query_width),
+    )
+
+    order = jnp.arange(tensor_size)[:, None, None]
+    upper_half = jnp.arange(2 * PAGE)[None, :, None] < PAGE
+    wide_counts = jnp.where(
+        jnp.logical_or(upper_half, seq_index > 0), counts_all.astype(F32), float(TOK)
+    )
+    wanted = jnp.where(upper_half, order <= tensor_index, order >= tensor_index)
+    starts_of = (
+        jnp.sum(jnp.where(wanted, wide_counts, 0.0), axis=(0, 1)) * (1.0 / PAGE)
     ).astype(jnp.int32)
     starts = jnp.sum(
         jnp.where(
@@ -396,7 +403,7 @@
         axis=0,
     )
     ctx, out_t = attention(
-        starts[None, :], projected[:tok_rows, :query_width], w_rows, kv_all
+        starts[None, :], projected, w_rows, kv_all
     )
     out_t = out_t.reshape(-1, query_width)
 
@@ -451,9 +458,10 @@
         produced.reshape(arrived.shape), "tensor", split_axis=0, concat_axis=0, tiled=True
     ).reshape(rows_flat.shape)
     tn = (((0,), (0,)), ((), ()))
-    routed_sum = lax.dot_general(
-        high, returned, tn, preferred_element_type=F32
-    ) + lax.dot_general(low, returned, tn, preferred_element_type=F32)
+    both_parts = lax.dot_general(
+        jnp.concatenate([high, low], axis=1), returned, tn, preferred_element_type=F32
+    )
+    routed_sum = both_parts[:tok_rows] + both_parts[tok_rows:]
     mixed = (residual.astype(F32) + routed_sum).astype(BF16)
     return (mixed, cache_pages)
 

time: 202 us -> 204 us (level)
  waiting for transfers between devices: 4.22 us -> 0.01 us
  other arithmetic: 4.91 us -> 8.35 us
  local copies, waits for them, and re-layouts: 11.1 us -> 13.4 us
    unnamed x29 -> x31, local copies, waits for them, and re-layouts: 6.47 us -> 10.7 us
    all_to_all x1, waiting for transfers between devices: 4.22 us -> 0.01 us  [body(): lax.all_to_all(produced.reshape(arrived.shape), 'tensor', split_axis=0, c...]
    dot_general x2 -> x1, matrix products: 5.23 us -> 2.46 us  [body(): lax.dot_general(jnp.concatenate([high, low], axis=1), returned, tn, prefe...]
  transfers between devices with their start and end apart: 1 -> 1, of which waited for: 1 -> 0; matrix products, arithmetic and copies ran while one was open for 3% -> 6% of each run, Pallas kernels for 0% -> 0%
where the time goes in v5:
time: 204 us; the launch traced here: 202 us
  Pallas kernels  91.1 us (45%)
  blocking collectives  36.7 us (18%)
  matrix products  26.8 us (13%)
  between operations  21.3 us (10%)
  local copies, waits for them, and re-layouts  13.4 us (7%)
  other arithmetic  8.35 us (4%)
  starting transfers between devices  4.73 us (2%)
    pallas_call x2, Pallas kernels, gather(): pl.pallas_call(functools.partial(gather_kernel, splits, len(sent), rows),...  69.1 us
    all_to_all x1, blocking collectives, body(): lax.all_to_all(outgoing, 'tensor', split_axis=0, concat_axis=0, tiled=True)  36.7 us
    pallas_call x1, Pallas kernels, attention(): pl.pallas_call(attention_kernel, out_shape=[jax.ShapeDtypeStruct((HEADS,...  22.1 us
    unnamed x31, local copies, waits for them, and re-layouts  10.7 us
    dot_general x1, matrix products, body(): jnp.dot(hidden, w_down[0], preferred_element_type=F32).astype(BF16)  9.12 us
    dot_general x1, matrix products, body(): lax.dot_general(normed, qkv_t, nt, preferred_element_type=F32).astype(BF16)  5.91 us
    all_to_all x1, starting transfers between devices, body(): lax.all_to_all(produced.reshape(arrived.shape), 'tensor', split_axis=0, c...  4.73 us
    dot_general x1, matrix products, body(): lax.dot_general(ctx.reshape(query_width, tok_rows), out_t, (((0,), (1,)),...  4.21 us
  transfers between devices with their start and end apart: 1, of which 0 were waited for; matrix products, arithmetic and copies ran while one was open for 6% of the time, Pallas kernels for 0%

profile of v5, /device:TPU:1, one launch (start us, length us, event | category | flops | bytes accessed | tf_op | source)
XLA Modules:
  0.0 202.5 jit_solution(7601041392823712033)
XLA Ops:
  0.6 0.0 copy-start
  0.7 0.6 iota_convert_fusion
  1.3 0.8 convert_reduce_fusion
  2.1 0.6 broadcast_in_dim.143.refs_2_
  2.7 34.7 %gather_0.1 = (bf16[32,64,1536]{2,1,0:T(8,128)(2,1)}, bf16[128,1536]{1,0:T(8,128)(2,1)}, bf16[16,128]{1,0:T(8,128)(2,1)}) custom-call(bf16[64,1536]{1,0:T(8,128)(2,1)} %bitcast.74, bf16[128,1536]{1,0:T(8,128)(2,1)} %refs_1_.1, bf16[16,128]{1,0:T(8,128)(2,1)} %broadcast_in_dim.143.refs_2_), custom_call_target="tpu_custom_call" | custom-call | tf_op jit(solution)/shard_map/gather_0/pallas_call | solution.py:227
  37.4 1.4 fusion.9
  38.8 1.4 bitcast_select_fusion.1.refs_1_
  40.2 0.1 broadcast_select_fusion
  40.3 5.9 %convolution_convert_fusion.2.refs_0_.q_ref = bf16[256,2048]{1,0:T(8,128)(2,1)} fusion(bf16[2048,1536]{1,0:T(8,128)(2,1)} %bitcast.81, f32[1536]{0:T(1024)} %param.15, f32[256]{0:T(256)S(1)} %add_rsqrt_fusion, bf16[128,1536]{1,0:T(8,128)(2,1)} %get-tuple-element.10, bf16[128,1536]{1,0:T(8,128)(2,1)} %refs_1_.1), kind=kOutput, calls=%fused_computation.2 | convolution fusion | flops 1613889536 | bytes 8133632 | tf_op jit(solution)/shard_map/dot_general | solution.py:376
  46.2 34.4 %gather_1.1 = (bf16[32,256,512]{2,1,0:T(8,128)(2,1)}, bf16[32,32,128]{2,1,0:T(8,128)(2,1)}, bf16[4,48,1536]{2,1,0:T(8,128)(2,1)}) custom-call(bf16[256,2048]{1,0:T(8,128)(2,1)} %convolution_convert_fusion.2.refs_0_.q_ref, bf16[32,128]{1,0:T(8,128)(2,1)} %bitcast_select_fusion.1.refs_1_, bf16[48,1536]{1,0:T(8,128)(2,1)} %bitcast.75), custom_call_target="tpu_custom_call" | custom-call | tf_op jit(solution)/shard_map/gather_1/pallas_call | solution.py:227
  80.5 1.2 select_reduce_fusion
  81.7 0.0 copy-done.11
  81.7 0.6 select_reduce_fusion.2
  82.3 22.1 %window_attention.1 = (bf16[12,128,128]{2,1,0:T(8,128)(2,1)}, bf16[32,48,1536]{2,1,0:T(8,128)(2,1)}) custom-call(s32[1,128]{1,0:T(1,128)} %bitcast.80, bf16[256,2048]{1,0:T(8,128)(2,1)} %convolution_convert_fusion.2.refs_0_.q_ref, bf16[4,48,1536]{2,1,0:T(8,128)(2,1)} %get-tuple-element.14.w_ref, bf16[32,256,512]{2,1,0:T(8,128)(2,1)} %get-tuple-element.15.kv_ref), custom_call_target="tpu_custom_call" | custom-call | tf_op jit(solution)/shard_map/window_attention/pallas_call | solution.py:325
  104.4 0.0 copy-done.1
  104.4 0.0 copy-start.5
  104.4 0.0 copy-start.9
  104.4 4.2 %multiply_reduce_fusion = (f32[128]{0:T(128)S(1)}, f32[128,1536]{1,0:T(8,128)S(1)}) fusion(bf16[1536,128]{1,0:T(8,128)(2,1)} %bitcast.73, bf16[1536,1536]{1,0:T(8,128)(2,1)} %bitcast.69, bf16[128,1536]{1,0:T(8,128)(2,1)S(1)} %copy-done.1), kind=kOutput, calls=%fused_computation.22 | convolution fusion | flops 605159296 | bytes 6291968 | tf_op jit(solution)/shard_map/dot_general | solution.py:428
  108.7 0.0 copy-done.5
  108.7 0.0 copy-start.4
  108.7 0.1 fusion.30
  108.8 0.0 copy-done.9
  108.8 0.1 eq.83
  108.9 0.0 copy-start.3
  109.0 0.2 fusion.28
  109.1 1.5 convolution_convert_fusion.1
  110.7 0.0 copy-start.10
  110.7 36.7 %all_to_all.10 = bf16[32,24,1536]{2,1,0:T(8,128)(2,1)S(1)} all-to-all(bf16[32,24,1536]{2,1,0:T(8,128)(2,1)S(1)} %bitcast.68), channel_id=1, replica_groups=mesh['seq'=8,'tensor'=32] {'tensor'}, dimensions={0} | all-to-all | bytes 4718592 | tf_op jit(solution)/shard_map/all_to_all | solution.py:451
  147.4 1.4 copy-done.2
  148.8 0.0 copy-done.10
  148.8 3.4 %fusion.3 = f32[768,768]{1,0:T(8,128)} fusion(bf16[768,1536]{1,0:T(8,128)(2,1)S(1)} %bitcast.71, bf16[1,1536,768]{2,1,0:T(8,128)(2,1)S(1)} %copy-done.10), kind=kOutput, calls=%fused_computation.7 | convolution fusion | flops 1811939328 | bytes 7077888 | tf_op jit(solution)/shard_map/dot_general | solution.py:454
  152.2 9.1 %convolution_convert_fusion = bf16[768,1536]{1,0:T(8,128)(2,1)} fusion(bf16[1,768,1536]{2,1,0:T(8,128)(2,1)S(1)} %copy-done, f32[768,768]{1,0:T(8,128)} %fusion.3, bf16[768,1536]{1,0:T(8,128)(2,1)} %bitcast.72, bf16[1,1536,768]{2,1,0:T(8,128)(2,1)} %param.21), kind=kOutput, calls=%fused_computation | convolution fusion | flops 3626827776 | bytes 11796480 | tf_op jit(solution)/shard_map/dot_general | solution.py:456
  161.4 4.7 %all-to-all-start.1 = ((bf16[32,24,1536]{2,1,0:T(8,128)(2,1)}), bf16[32,24,1536]{2,1,0:T(8,128)(2,1)}, u32[]{:S(2)}, u32[]{:S(2)}) async-start(bf16[32,24,1536]{2,1,0:T(8,128)(2,1)} %bitcast.70), calls=%async_computation.1 | async-start | bytes 4718592 | tf_op jit(solution)/shard_map/all_to_all | solution.py:457
  166.1 0.2 select_reduce_fusion.3
  166.3 0.7 fusion.34
  187.4 0.2 fusion.24
  187.6 0.9 fusion.25
  188.5 1.3 constant_dynamic-update-slice_fusion.7
  189.9 1.3 constant_dynamic-update-slice_fusion.6
  191.2 1.3 constant_dynamic-update-slice_fusion.5
  192.5 1.3 constant_dynamic-update-slice_fusion.4
  193.8 1.3 constant_dynamic-update-slice_fusion.3
  195.2 1.3 constant_dynamic-update-slice_fusion.2
  196.5 1.3 constant_dynamic-update-slice_fusion.1
  197.8 1.3 constant_dynamic-update-slice_fusion
  199.1 0.0 all-to-all-done.1
  199.1 2.5 %fusion.19 = f32[256,1536]{1,0:T(8,128)S(1)} fusion(bf16[768,1536]{1,0:T(8,128)(2,1)} %bitcast.18, bf16[768,128]{1,0:T(8,128)(2,1)S(1)} %fusion.25, bf16[768,128]{1,0:T(8,128)(2,1)S(1)} %fusion.24), kind=kOutput, calls=%fused_computation.26 | convolution fusion | flops 604766208 | bytes 4325376 | tf_op jit(solution)/shard_map/dot_general | solution.py:461
  201.6 0.9 fusion.14
  (22 shorter events, 0.1 us)
Async XLA Ops:
  0.6 151.6 %copy-start = (bf16[1,768,1536]{2,1,0:T(8,128)(2,1)S(1)}, bf16[1,768,1536]{2,1,0:T(8,128)(2,1)}, u32[]{:S(2)}) copy-start(bf16[1,768,1536]{2,1,0:T(8,128)(2,1)} %param.23) | copy-start | bytes 7077892
  40.3 41.5 %copy-start.11 = (s32[128]{0:T(128)S(1)}, s32[128]{0:T(128)}, u32[]{:S(2)}) copy-start(s32[128]{0:T(128)} %param.13) | copy-start | bytes 1540
  82.3 22.1 %copy-start.1 = (bf16[128,1536]{1,0:T(8,128)(2,1)S(1)}, bf16[128,1536]{1,0:T(8,128)(2,1)}, u32[]{:S(2)}) copy-start(bf16[128,1536]{1,0:T(8,128)(2,1)} %refs_1_.1) | copy-start | bytes 1179652
  104.4 4.2 %copy-start.5 = (s32[128,4]{0,1:T(4,128)S(1)}, s32[128,4]{0,1:T(4,128)}, u32[]{:S(2)}) copy-start(s32[128,4]{0,1:T(4,128)} %param.19) | copy-start | bytes 6148
  104.4 4.4 %copy-start.9 = (f32[24]{0:T(128)S(1)}, f32[24]{0:T(128)}, u32[]{:S(2)}) copy-start(f32[24]{0:T(128)} %iota_convert_fusion) | copy-start | bytes 292
  108.7 78.7 %copy-start.4 = (pred[32,128]{1,0:T(8,128)(4,1)}, pred[32,128]{1,0:T(8,128)(4,1)S(1)}, u32[]{:S(2)}) copy-start(pred[32,128]{1,0:T(8,128)(4,1)S(1)} %fusion.29) | copy-start | bytes 12292
  108.9 78.4 %copy-start.3 = (f32[768]{0:T(1024)}, f32[768]{0:T(1024)S(1)}, u32[]{:S(2)}) copy-start(f32[768]{0:T(1024)S(1)} %eq.83) | copy-start | bytes 9220
  110.7 38.1 %copy-start.10 = (bf16[1,1536,768]{2,1,0:T(8,128)(2,1)S(1)}, bf16[1,1536,768]{2,1,0:T(8,128)(2,1)}, u32[]{:S(2)}) copy-start(bf16[1,1536,768]{2,1,0:T(8,128)(2,1)} %param.22) | copy-start | bytes 7077892
  147.4 1.4 copy-start.2
  161.4 4.8 %copy-start.8 = (s32[1,256]{1,0:T(1,128)S(1)}, s32[1,256]{1,0:T(1,128)}, u32[]{:S(2)}) copy-start(s32[1,256]{1,0:T(1,128)} %param.14) | copy-start | bytes 3076
  161.4 26.0 %copy-start.6 = (s32[128,4]{0,1:T(4,128)S(1)}, s32[128,4]{0,1:T(4,128)}, u32[]{:S(2)}) copy-start(s32[128,4]{0,1:T(4,128)} %param.19) | copy-start | bytes 6148
  161.4 26.0 %copy-start.7 = (f32[128,4]{0,1:T(4,128)S(1)}, f32[128,4]{0,1:T(4,128)}, u32[]{:S(2)}) copy-start(f32[128,4]{0,1:T(4,128)} %param.20) | copy-start | bytes 6148
  161.4 37.8 %all-to-all-start.1 = ((bf16[32,24,1536]{2,1,0:T(8,128)(2,1)}), bf16[32,24,1536]{2,1,0:T(8,128)(2,1)}, u32[]{:S(2)}, u32[]{:S(2)}) async-start(bf16[32,24,1536]{2,1,0:T(8,128)(2,1)} %bitcast.70), calls=%async_computation.1 | async-start | bytes 4718592 | tf_op jit(solution)/shard_map/all_to_all | solution.py:457
